TPU v7x, 512 devices: a whole 4x8x8 slice. The times are simulated.
512 devices in a mesh: img: 8 (over y_lo, core), cin: 8 (over x, y_hi), cout: 8 (over z).
Axes of the slice: x: 4, y: 8 (y_hi: 2, y_lo: 4; y = y_hi * 4 + y_lo), z: 8, core: 2. Of those that a mesh axis runs over, the one named last changes fastest.
Arguments:
- maps: bfloat16 [2, 8, 14, 14, 1024], P(None, 'img'), may hold values from -6 to 6
- w_first: bfloat16 [3, 3, 1024, 1024], P(None, None, 'cin', 'cout'), may hold values from -0.09375 to 0.09375
- w_reduce: bfloat16 [3, 3, 1024, 8192], P(None, None, 'img', ('cin', 'cout')), may hold values from -0.09375 to 0.09375
- w_wide: bfloat16 [3, 3, 8192, 8192], P(None, None, 'cin', ('img', 'cout')), may hold values from -0.03125 to 0.03125
Outputs:
- wide_out: bfloat16 [2, 8, 7, 7, 8192], P(None, 'cin', None, None, ('img', 'cout'))
All inputs are finite; a program needn't handle non-finite values.
Results may differ from a plain program's by a relative error of at most 0.014.
Values may be sent and summed in bfloat16 or wider, within the bound.
No kernel may reach another device: no remote copies, remote signals or barrier semaphores. Data moves between devices by JAX's collectives and lax.ppermute only.
A program may use at most 64 MiB of HBM per device.

v0:
```python
import jax
import jax.numpy as jnp
from jax import lax
from jax.sharding import PartitionSpec as P


def conv_block(padded, weight_flat, size, step):
    channels = padded.shape[3]
    windows = []
    for row_tap in range(3):
        for col_tap in range(3):
            windows.append(
                padded[
                    :,
                    row_tap : row_tap + step * (size - 1) + 1 : step,
                    col_tap : col_tap + step * (size - 1) + 1 : step,
                    :,
                ]
            )
    table = jnp.concatenate(windows, axis=3).reshape(-1, 9 * channels)
    total = jnp.dot(table, weight_flat, preferred_element_type=jnp.float32)
    return total.reshape(padded.shape[0], size, size, weight_flat.shape[1])


def conv_taps(padded, weight, size, step):
    count = padded.shape[0]
    channels = padded.shape[3]
    weight_flat = weight.reshape(9 * channels, weight.shape[3])
    group = 1
    for trial in range(1, 9):
        if count % trial == 0:
            group = trial
    blocks = padded.reshape(count // group, group, padded.shape[1], padded.shape[2], channels)
    results = lax.map(lambda block: conv_block(block, weight_flat, size, step), blocks)
    return results.reshape(count, size, size, weight.shape[3])


def pad_map(values):
    return jnp.pad(values, ((0, 0), (1, 1), (1, 1), (0, 0)))


def local(maps, w_first, w_reduce, w_wide):
    batches = maps.shape[0]
    side = maps.shape[2]
    half = side // 2
    in_block = w_first.shape[2]
    out_block = w_first.shape[3]
    flat = maps.reshape(-1, side, side, maps.shape[4])
    in_part = lax.dynamic_slice_in_dim(flat, lax.axis_index("cin") * in_block, in_block, 3)
    first_terms = conv_taps(pad_map(jnp.maximum(in_part, 0)), w_first, side, 1)
    first_terms = first_terms.reshape(batches, maps.shape[1], side, side, out_block)
    summed = lax.psum(first_terms, "cin")
    own_part = lax.dynamic_slice_in_dim(maps, lax.axis_index("cout") * out_block, out_block, 4)
    segment_maps = (own_part.astype(jnp.float32) + summed).astype(jnp.bfloat16)
    whole = lax.all_gather(segment_maps, "cout", axis=4, tiled=True)
    by_channel = lax.all_to_all(whole, "img", split_axis=4, concat_axis=1, tiled=True)
    images = by_channel.shape[1]
    rect_segment = jnp.maximum(by_channel, 0).reshape(-1, side, side, by_channel.shape[4])
    reduced = conv_taps(pad_map(rect_segment), w_reduce, half, 2).reshape(
        batches, images, half, half, w_reduce.shape[3]
    )
    out_width = w_wide.shape[3]
    summed_wide = lax.psum(reduced, "img")
    narrow = jnp.maximum(summed_wide, 0.0).astype(jnp.bfloat16)
    gathered = lax.all_gather(narrow, "cout", axis=4, tiled=True)
    flat_all = gathered.reshape(-1, half, half, gathered.shape[4])
    partial_value = conv_taps(pad_map(flat_all), w_wide, half, 1)
    partial_value = partial_value.reshape(batches, images, half, half, out_width)
    result = lax.psum_scatter(
        partial_value.astype(jnp.bfloat16), "cin", scatter_dimension=1, tiled=True
    )
    return result


def solution(mesh):
    in_specs = (
        P(None, "img", None, None, None),
        P(None, None, "cin", "cout"),
        P(None, None, "img", ("cin", "cout")),
        P(None, None, "cin", ("img", "cout")),
    )
    out_specs = P(None, "cin", None, None, ("img", "cout"))
    return jax.shard_map(local, mesh=mesh, in_specs=in_specs, out_specs=out_specs, check_vma=False)
```

profile of v0, /device:TPU:64, one launch (start us, length us, event | category | flops | bytes accessed | tf_op | source)
XLA Modules:
  0.0 461.7 jit_solution(14591765025077755233)
XLA Ops:
  6.5 1.1 constant_dynamic-slice_fusion.2
  7.8 0.1 slice_dynamic-update-slice_fusion.23
  7.8 0.1 slice_dynamic-update-slice_fusion.22
  8.0 0.1 slice_dynamic-update-slice_fusion.21
  8.0 0.1 slice_dynamic-update-slice_fusion.20
  8.1 0.1 slice_dynamic-update-slice_fusion.18
  8.2 1.1 convolution_bitcast_fusion.1
  9.3 116.6 %all-reduce.8.cloned.1.call-done = f32[2,1,14,14,128]{4,3,2,0,1:T(8,128)} async-done(((f32[2,1,14,14,128]{4,3,2,0,1:T(8,128)}), f32[2,1,14,14,128]{4,3,2,0,1:T(8,128)}) %all-reduce.8.cloned.1.call-update) | async-done | bytes 200720 | tf_op jit(solution)/shard_map/psum | solution.py:52
  126.0 1.0 add_convert_fusion
  126.9 26.5 %all_gather.6 = bf16[2,1,14,14,1024]{4,3,2,0,1:T(8,128)(2,1)S(1)} all-gather(bf16[2,1,14,14,128]{4,3,2,0,1:T(8,128)(2,1)S(1)} %add_convert_fusion), channel_id=1, replica_groups=mesh['img'=8,'cin'=8,'cout'=8] {'cout'}, dimensions={4}, use_global_device_ids=true | all-gather | bytes 903168 | tf_op jit(solution)/shard_map/all_gather | solution.py:55
  153.5 12.4 %copy.42 = bf16[2,1,14,14,1024]{3,0,2,1,4:T(2,128)(2,1)} copy(bf16[2,1,14,14,1024]{4,3,2,0,1:T(8,128)(2,1)S(1)} %all_gather.6) | data formatting | bytes 1605632 | tf_op jit(solution)/shard_map/all_gather | solution.py:55
  165.8 12.8 %reshape.68 = bf16[8,2,25088]{2,1,0:T(2,128)(2,1)} reshape(bf16[1024,1,14,2,14]{4,3,2,1,0:T(2,128)(2,1)} %bitcast.84) | data formatting | bytes 1605632
  178.7 3.5 all-to-all-start
  182.3 21.2 %all-to-all-done = bf16[8,2,25088]{2,1,0:T(2,128)(2,1)S(1)} async-done(((bf16[8,2,25088]{2,1,0:T(2,128)(2,1)}), bf16[8,2,25088]{2,1,0:T(2,128)(2,1)S(1)}, u32[]{:S(2)}, u32[]{:S(2)}) %all-to-all-start) | async-done | bytes 802848 | tf_op jit(solution)/shard_map/all_to_all | solution.py:56
  203.4 19.8 %reshape.69 = bf16[1024,1,14,2,14]{4,3,2,1,0:T(2,128)(2,1)} reshape(bf16[8,2,25088]{2,1,0:T(2,128)(2,1)S(1)} %all-to-all-done) | data formatting | bytes 1605632
  223.2 17.3 %copy.43 = bf16[2,1,14,14,1024]{4,0,3,2,1:T(2,128)(2,1)S(1)} copy(bf16[2,1,14,14,1024]{3,0,2,1,4:T(2,128)(2,1)} %bitcast.85) | data formatting | bytes 1605632 | tf_op jit(solution)/shard_map/all_to_all | solution.py:56
  240.5 0.7 broadcast_maximum_fusion
  241.2 0.5 max.33
  241.7 1.2 pad_bitcast_fusion.1
  242.9 4.0 while.26
  242.9 1.2 dynamic-slice_bitcast_fusion.6
  244.5 0.4 fusion.26
  245.0 1.1 dynamic-slice_bitcast_fusion.6
  246.4 0.4 fusion.26
  246.9 31.9 %all-reduce.11 = bf16[2,8,7,7,128]{4,1,0,3,2:T(8,128)(2,1)S(1)} all-reduce(f32[2,8,7,7,128]{4,1,0,3,2:T(8,128)S(1)} %get-tuple-element.61), channel_id=1, replica_groups=mesh['img'=8,'cin'=8,'cout'=8] {'img'}, use_global_device_ids=true, to_apply=%region_3.4 | all-reduce | flops 100352 | bytes 602112 | tf_op jit(solution)/shard_map/psum | solution.py:63
  278.8 0.7 maximum_convert_fusion
  279.6 41.6 %all-gather.2.cloned.1.call-done = bf16[2,8,7,7,1024]{4,1,0,3,2:T(8,128)(2,1)} async-done(((bf16[2,8,7,7,128]{4,1,0,3,2:T(8,128)(2,1)}), bf16[2,8,7,7,1024]{4,1,0,3,2:T(8,128)(2,1)}) %all-gather.2.cloned.1.call-update) | async-done | bytes 1605648 | tf_op jit(solution)/shard_map/all_gather | solution.py:65
  321.2 3.3 pad_bitcast_fusion
  324.5 17.2 %while.27 = (s32[]{:T(128)}, bf16[2,8,7,7,128]{4,0,3,2,1:T(2,128)(2,1)S(1)}, bf16[2,8,9,9,1024]{4,1,0,3,2:T(8,128)(2,1)}, bf16[9216,128]{1,0:T(8,128)(2,1)S(1)}) while((s32[]{:T(128)}, bf16[2,8,7,7,128]{4,0,3,2,1:T(2,128)(2,1)S(1)}, bf16[2,8,9,9,1024]{4,1,0,3,2:T(8,128)(2,1)}, bf16[9216,128]{1,0:T(8,128)(2,1)S(1)}) %tuple.60), condition=%wide.region_5.6_spmd.clone, body=%wide.region_4.5_spmd.sunk.clone | while | flops 924844032 | bytes 27191356 | solution.py:34
  324.5 1.4 dynamic-slice_bitcast_fusion.7
  326.0 0.1 slice_dynamic-update-slice_fusion.72
  326.1 0.1 slice_dynamic-update-slice_fusion.73
  326.3 0.1 slice_dynamic-update-slice_fusion.76
  326.3 0.1 slice_dynamic-update-slice_fusion.77
  326.5 2.0 fusion.29
  328.6 0.2 copy.72
  328.7 4.4 dynamic_update_slice.16
  333.1 1.4 dynamic-slice_bitcast_fusion.7
  334.7 0.1 slice_dynamic-update-slice_fusion.73
  334.8 0.1 slice_dynamic-update-slice_fusion.74
  334.9 0.1 slice_dynamic-update-slice_fusion.77
  335.1 2.0 fusion.29
  337.2 0.2 copy.72
  337.3 4.4 dynamic_update_slice.16
  341.8 0.7 copy-done.3
  342.5 1.3 dynamic-slice.2
  343.7 109.5 %all-reduce.10.cloned.1.call-done = bf16[2,8,7,7,128]{4,0,3,2,1:T(2,128)(2,1)} async-done(((bf16[2,8,7,7,128]{4,0,3,2,1:T(2,128)(2,1)}), bf16[2,8,7,7,128]{4,0,3,2,1:T(2,128)(2,1)}) %all-reduce.10.cloned.1.call-update) | async-done | bytes 200720
  453.3 1.9 constant_dynamic-slice_fusion
  (49 shorter events, 1.6 us)
Async XLA Ops:
  6.5 1.6 copy-start
  6.5 119.4 %all-reduce.8.cloned.1.call-start = ((), (), s32[]{:S(2)}) async-start(), calls=%async_computation.1 | async-start | bytes 458752 | tf_op jit(solution)/shard_map/psum | solution.py:52
  178.7 24.8 %all-to-all-start = ((bf16[8,2,25088]{2,1,0:T(2,128)(2,1)}), bf16[8,2,25088]{2,1,0:T(2,128)(2,1)S(1)}, u32[]{:S(2)}, u32[]{:S(2)}) async-start(bf16[8,2,25088]{2,1,0:T(2,128)(2,1)} %reshape.68), calls=%async_computation | async-start | bytes 1605632 | tf_op jit(solution)/shard_map/all_to_all | solution.py:56
  182.2 139.0 %all-gather.2.cloned.1.call-start = ((), (), s32[]{:S(2)}) async-start(), calls=%async_computation.2 | async-start | bytes 1806336 | tf_op jit(solution)/shard_map/all_gather | solution.py:65
  223.2 19.7 %copy-start.2 = (bf16[3,3,128,128]{3,2,1,0:T(8,128)(2,1)S(1)}, bf16[3,3,128,128]{3,2,1,0:T(8,128)(2,1)}, u32[]{:S(2)}) copy-start(bf16[3,3,128,128]{3,2,1,0:T(8,128)(2,1)} %param.10) | copy-start | bytes 884740
  242.9 81.6 %copy-start.1 = (bf16[3,3,1024,128]{3,2,1,0:T(8,128)(2,1)S(1)}, bf16[3,3,1024,128]{3,2,1,0:T(8,128)(2,1)}, u32[]{:S(2)}) copy-start(bf16[3,3,1024,128]{3,2,1,0:T(8,128)(2,1)} %param.11) | copy-start | bytes 7077892
  279.5 173.7 %all-reduce.10.cloned.1.call-start = ((), (), s32[]{:S(2)}) async-start(), calls=%async_computation.3 | async-start | bytes 401408
  341.8 0.7 copy-start.3
Sparse Core Ops, SparseCore 0:
  10.3 115.6 all-reduce.7
  279.6 41.5 all-gather.1
  342.6 110.6 all-reduce.9
where the time goes:
time: 463 us; the launch traced here: 462 us
  waiting for transfers between devices  289 us (62%)
  local copies, waits for them, and re-layouts  88.5 us (19%)
  blocking collectives  58.4 us (13%)
  between operations  13.3 us (3%)
  matrix products  6.06 us (1%)
    psum x1, waiting for transfers between devices, local(): summed = lax.psum(first_terms, 'cin')  117 us
    unnamed x4, waiting for transfers between devices  110 us
    all_gather x1, waiting for transfers between devices, local(): gathered = lax.all_gather(narrow, 'cout', axis=4, tiled=True)  41.6 us
    unnamed x19, local copies, waits for them, and re-layouts  36.8 us
    psum x1, blocking collectives, local(): summed_wide = lax.psum(reduced, 'img')  31.9 us
    all_gather x1, blocking collectives, local(): whole = lax.all_gather(segment_maps, 'cout', axis=4, tiled=True)  26.5 us
    all_to_all x1, waiting for transfers between devices, local(): lax.all_to_all(whole, 'img', split_axis=4, concat_axis=1, tiled=True)  21.2 us
    all_to_all x1, local copies, waits for them, and re-layouts, local(): lax.all_to_all(whole, 'img', split_axis=4, concat_axis=1, tiled=True)  17.3 us
  transfers between devices with their start and end apart: 4, of which 4 were waited for; matrix products, arithmetic and copies ran while one was open for 0% of the time, Pallas kernels for 0%

commit v1 on v0

v1 whole, which is shorter than its diff:
```python
import jax
import jax.numpy as jnp
from jax import lax
from jax.sharding import Mesh, PartitionSpec as P

YL, CORE, X, YH, Z = "yl", "core", "x", "yh", "z"
SIZES = (4, 2, 4, 2, 8)
IMG_Z_TURN = [(i * 8 + o, o * 8 + i) for i in range(8) for o in range(8)]
SWAP = [(0, 1), (1, 0)]
BF = jnp.bfloat16
F32 = jnp.float32


def exchange(values, axes):
    return lax.all_to_all(values, axes, 0, 0, tiled=True)


def both_cores(weight):
    other = lax.ppermute(weight, CORE, SWAP)
    first = lax.axis_index(CORE) == 0
    return jnp.concatenate([jnp.where(first, weight, other), jnp.where(first, other, weight)], axis=3)


def parity_planes(values):
    n, _, _, c = values.shape
    return values.reshape(n, 7, 2, 7, 2, c).transpose(2, 4, 0, 1, 3, 5).reshape(4, n, 7, 7, c)


def first_conv(part, weight):
    n, _, _, c = part.shape
    padded = jnp.pad(part, ((0, 0), (1, 1), (1, 1), (0, 0)))
    cells = padded.reshape(n, 8, 2, 8, 2, c).transpose(2, 4, 0, 1, 3, 5)
    cells = jnp.pad(cells, ((0, 0), (0, 0), (0, 0), (0, 0), (1, 0), (0, 0)))
    planes = []
    for row in range(2):
        for col in range(2):
            taps = []
            for a in range(3):
                for b in range(3):
                    i, qi = divmod(row + a, 2)
                    j, qj = divmod(col + b, 2)
                    taps.append(cells[qi, qj, :, i : i + 7, j : j + 8])
            planes.append(jnp.concatenate(taps, axis=3).reshape(n * 56, 9 * c))
    table = jnp.concatenate(planes, axis=0)
    return jnp.dot(table, weight.reshape(9 * c, -1), preferred_element_type=F32)


def reduce_conv(planes, weight):
    n, c = planes.shape[1], planes.shape[4]
    taps = []
    for a in range(3):
        for b in range(3):
            plane = planes[2 * ((a + 1) % 2) + (b + 1) % 2]
            if a == 0:
                plane = jnp.pad(plane[:, :6], ((0, 0), (1, 0), (0, 0), (0, 0)))
            if b == 0:
                plane = jnp.pad(plane[:, :, :7], ((0, 0), (0, 0), (1, 0), (0, 0)))
            taps.append(plane)
    table = jnp.concatenate(taps, axis=3).reshape(n * 56, 9 * c)
    return jnp.dot(table, weight.reshape(9 * c, -1), preferred_element_type=F32)


def wide_conv(maps, weight):
    n, groups, _, _, c = maps.shape
    padded = jnp.pad(maps, ((0, 0), (0, 0), (1, 1), (1, 1), (0, 0)))
    taps = []
    for a in range(3):
        for b in range(3):
            for g in range(groups):
                taps.append(padded[:, g, a : a + 7, b : b + 8])
    table = jnp.concatenate(taps, axis=3).reshape(n * 56, 9 * groups * c)
    return jnp.dot(table, weight.reshape(9 * groups * c, -1), preferred_element_type=F32)


def real_columns(values):
    column = lax.broadcasted_iota(jnp.int32, values.shape, values.ndim - 2)
    return jnp.where(column > 0, values, jnp.zeros_like(values))


def local(maps, w_first, w_reduce, w_wide):
    core = lax.axis_index(CORE)
    plane = lax.axis_index(X)
    in_block = lax.axis_index(X) * 2 + lax.axis_index(YH)
    out_block = lax.axis_index(Z)
    images = maps.reshape(2, 14, 14, 1024)
    part = lax.dynamic_slice_in_dim(images, in_block * 128, 128, 3)

    first = first_conv(jnp.maximum(part, 0), w_first).astype(BF).reshape(4, 1, 112, 128)
    first = exchange(jnp.broadcast_to(first, (4, 2, 112, 128)).reshape(8, 112, 128), (X, YH))
    summed = first.astype(F32).sum(0).reshape(2, 7, 8, 128)

    turned = lax.ppermute(w_reduce, (YL, CORE, Z), IMG_Z_TURN)
    weight_reduce = both_cores(turned)
    weight_wide = both_cores(w_wide)

    own = lax.dynamic_slice_in_dim(images, out_block * 128, 128, 3)
    own = lax.dynamic_index_in_dim(parity_planes(own), plane, 0, keepdims=False)
    own = jnp.pad(own, ((0, 0), (0, 0), (1, 0), (0, 0)))
    segment = (own.astype(F32) + summed).astype(BF)
    segment = real_columns(jnp.maximum(segment, 0)).reshape(2, 56, 128)

    send = jnp.broadcast_to(segment[None, :, None], (4, 2, 4, 56, 128)).reshape(32, 56, 128)
    planes = exchange(send, (YL, CORE, X)).reshape(8, 4, 7, 8, 128).transpose(1, 0, 2, 3, 4)

    reduced = reduce_conv(planes, weight_reduce).astype(BF).reshape(8, 56, 256)
    reduced = exchange(reduced, (Z,)).astype(F32).sum(0)
    narrow = real_columns(jnp.maximum(reduced, 0.0).astype(BF).reshape(7, 8, 256)).reshape(56, 256)

    gathered = exchange(jnp.broadcast_to(narrow, (32, 56, 256)), (YL, Z)).reshape(4, 8, 7, 8, 256)
    wide = wide_conv(gathered.transpose(1, 0, 2, 3, 4), weight_wide).astype(BF)

    wide = wide.reshape(8, 56, 2, 128).transpose(2, 0, 1, 3).reshape(16, 56, 128)
    wide = exchange(wide, (CORE, X, YH)).reshape(2, 8, 7, 8, 128)
    total = wide.astype(F32).sum(1).astype(BF)
    return total[:, None, :, 1:, :]


def solution(mesh):
    fine = Mesh(mesh.devices.reshape(SIZES), (YL, CORE, X, YH, Z))
    img, cin = (YL, CORE), (X, YH)
    in_specs = (
        P(None, img, None, None, None),
        P(None, None, cin, Z),
        P(None, None, img, cin + (Z,)),
        P(None, None, cin, img + (Z,)),
    )
    out_specs = P(None, cin, None, None, img + (Z,))
    return jax.shard_map(local, mesh=fine, in_specs=in_specs, out_specs=out_specs, check_vma=False)
```

time: 463 us -> 135 us (0.29)
  the two profiles are of different devices: /device:TPU:64 before, /device:TPU:72 now
where the time goes in v1:
time: 135 us
  waiting for transfers between devices  52.3 us (39%)
  starting transfers between devices  37.8 us (28%)
  blocking collectives  23.9 us (18%)
  local copies, waits for them, and re-layouts  9.91 us (7%)
  other arithmetic  5.82 us (4%)
  matrix products  3.89 us (3%)
    all_to_all x4, waiting for transfers between devices, exchange(): return lax.all_to_all(values, axes, 0, 0, tiled=True)  51.9 us
    all_to_all x4, starting transfers between devices, exchange(): return lax.all_to_all(values, axes, 0, 0, tiled=True)  27.1 us
    all_to_all x1, blocking collectives, exchange(): return lax.all_to_all(values, axes, 0, 0, tiled=True)  23.9 us
    ppermute x2, starting transfers between devices, both_cores(): other = lax.ppermute(weight, CORE, SWAP)  6.55 us
    ppermute x1, starting transfers between devices, local(): turned = lax.ppermute(w_reduce, (YL, CORE, Z), IMG_Z_TURN)  4.22 us
    concatenate x2, other arithmetic, both_cores(): jnp.concatenate([jnp.where(first, weight, other), jnp.where(first, other,...  2.79 us
    select_n x2, other arithmetic, both_cores(): jnp.where(first, weight, other)  2.73 us
    unnamed x78, local copies, waits for them, and re-layouts  2.71 us
  transfers between devices with their start and end apart: 7, of which 5 were waited for; matrix products, arithmetic and copies ran while one was open for 7% of the time, Pallas kernels for 0%

profile of v1, /device:TPU:72, one launch (start us, length us, event | category | flops | bytes accessed | tf_op | source)
XLA Modules:
  0.0 134.5 jit_solution(5181741734381461842)
XLA Ops:
  0.0 0.0 copy-start
  0.0 0.0 copy-start.1
  0.0 1.1 constant_dynamic-slice_fusion.1
  1.2 0.4 pad_slice_fusion.40
  1.6 0.2 fusion.13
  2.5 0.0 copy-done
  2.5 0.4 convolution_convert_fusion.2
  3.0 0.7 broadcast_in_dim.24
  3.7 8.7 %all-to-all-start = ((bf16[8,112,128]{2,1,0:T(8,128)(2,1)}), bf16[8,112,128]{2,1,0:T(8,128)(2,1)S(1)}, u32[]{:S(2)}, u32[]{:S(2)}) async-start(bf16[8,112,128]{2,1,0:T(8,128)(2,1)} %bitcast.10), calls=%async_computation | async-start | bytes 458752 | tf_op jit(solution)/shard_map/all_to_all | solution.py:15
  12.3 0.0 copy-done.1
  12.3 4.2 %collective-permute-start = (bf16[3,3,128,128]{3,2,1,0:T(8,128)(2,1)S(1)}, bf16[3,3,128,128]{3,2,1,0:T(8,128)(2,1)S(1)}, u32[]{:S(2)}, u32[]{:S(2)}) collective-permute-start(bf16[3,3,128,128]{3,2,1,0:T(8,128)(2,1)S(1)} %copy-done.1), channel_id=1, source_target_pairs={{0,0},{1,64},{2,128},{3,192},{4,256},{5,320},{6,384},{7,448},{64,1... | collective-permute-start | bytes 884744 | tf_op jit(solution)/shard_map/ppermute | solution.py:92
  16.6 0.1 copy.25
  16.7 8.9 %all-to-all-done = bf16[8,112,128]{2,1,0:T(8,128)(2,1)S(1)} async-done(((bf16[8,112,128]{2,1,0:T(8,128)(2,1)}), bf16[8,112,128]{2,1,0:T(8,128)(2,1)S(1)}, u32[]{:S(2)}, u32[]{:S(2)}) %all-to-all-start) | async-done | bytes 229408 | tf_op jit(solution)/shard_map/all_to_all | solution.py:15
  25.7 0.1 broadcast_select_fusion.4
  25.8 0.8 broadcast_in_dim.26
  26.6 4.8 %all-to-all-start.1 = ((bf16[32,56,128]{2,1,0:T(8,128)(2,1)}), bf16[32,56,128]{2,1,0:T(8,128)(2,1)S(1)}, u32[]{:S(2)}, u32[]{:S(2)}) async-start(bf16[32,56,128]{2,1,0:T(8,128)(2,1)} %bitcast.13), calls=%async_computation.1 | async-start | bytes 917504 | tf_op jit(solution)/shard_map/all_to_all | solution.py:15
  31.4 0.4 collective-permute-done
  31.8 4.6 %collective-permute-start.1 = (bf16[3,3,128,128]{3,2,1,0:T(8,128)(2,1)S(1)}, bf16[3,3,128,128]{3,2,1,0:T(8,128)(2,1)S(1)}, u32[]{:S(2)}, u32[]{:S(2)}) collective-permute-start(bf16[3,3,128,128]{3,2,1,0:T(8,128)(2,1)S(1)} %collective-permute-done), channel_id=1, source_target_pairs={{0,64},{64,0},{1,65},{65,1},{2,66},{66,2},{3,67},{67,3},{4,68},{68... | collective-permute-start | bytes 884744 | tf_op jit(solution)/shard_map/ppermute | solution.py:19
  36.4 1.9 %collective-permute-start.2 = (bf16[3,3,1024,128]{3,2,1,0:T(8,128)(2,1)}, bf16[3,3,1024,128]{3,2,1,0:T(8,128)(2,1)}, u32[]{:S(2)}, u32[]{:S(2)}) collective-permute-start(bf16[3,3,1024,128]{3,2,1,0:T(8,128)(2,1)} %param.7), channel_id=1, source_target_pairs={{0,64},{64,0},{1,65},{65,1},{2,66},{66,2},{3,67},{67,3},{4,68},{68... | collective-permute-start | bytes 7077896 | tf_op jit(solution)/shard_map/ppermute | solution.py:19
  38.4 0.0 collective-permute-done.1
  38.4 0.1 pad_maximum_fusion.1
  38.5 14.5 %all-to-all-done.1 = bf16[32,56,128]{2,1,0:T(8,128)(2,1)S(1)} async-done(((bf16[32,56,128]{2,1,0:T(8,128)(2,1)}), bf16[32,56,128]{2,1,0:T(8,128)(2,1)S(1)}, u32[]{:S(2)}, u32[]{:S(2)}) %all-to-all-start.1) | async-done | bytes 458784 | tf_op jit(solution)/shard_map/all_to_all | solution.py:15
  53.0 0.1 fusion.12
  53.6 1.2 convolution_convert_fusion
  54.8 7.5 %all-to-all-start.2 = ((bf16[8,56,256]{2,1,0:T(8,128)(2,1)}), bf16[8,56,256]{2,1,0:T(8,128)(2,1)S(1)}, u32[]{:S(2)}, u32[]{:S(2)}) async-start(bf16[8,56,256]{2,1,0:T(8,128)(2,1)} %bitcast.30), calls=%async_computation.2 | async-start | bytes 458752 | tf_op jit(solution)/shard_map/all_to_all | solution.py:15
  62.3 0.1 iota.18
  62.4 9.7 %all-to-all-done.2 = bf16[8,56,256]{2,1,0:T(8,128)(2,1)S(1)} async-done(((bf16[8,56,256]{2,1,0:T(8,128)(2,1)}), bf16[8,56,256]{2,1,0:T(8,128)(2,1)S(1)}, u32[]{:S(2)}, u32[]{:S(2)}) %all-to-all-start.2) | async-done | bytes 229408 | tf_op jit(solution)/shard_map/all_to_all | solution.py:15
  72.2 0.1 fusion.9
  72.3 1.0 broadcast_in_dim.28
  73.3 6.1 %all-to-all-start.3 = ((bf16[32,56,256]{2,1,0:T(8,128)(2,1)}), bf16[32,56,256]{2,1,0:T(8,128)(2,1)S(1)}, u32[]{:S(2)}, u32[]{:S(2)}) async-start(bf16[32,56,256]{2,1,0:T(8,128)(2,1)} %broadcast_in_dim.28), calls=%async_computation.3 | async-start | bytes 1835008 | tf_op jit(solution)/shard_map/all_to_all | solution.py:15
  79.4 0.0 collective-permute-done.2
  79.4 2.7 %broadcast_select_fusion.1 = (bf16[3,3,1024,128]{3,2,1,0:T(8,128)(2,1)S(1)}, bf16[3,3,1024,128]{3,2,1,0:T(8,128)(2,1)S(1)}) fusion(bf16[3,3,1024,128]{3,2,1,0:T(8,128)(2,1)} %param.7, bf16[3,3,1024,128]{3,2,1,0:T(8,128)(2,1)} %collective-permute-done.2, pred[]{:T(512)S(6)} %eq.4), kind=kLoop, calls=%fused_computation.34 | loop fusion | flops 2359296 | bytes 9437185 | tf_op jit(solution)/shard_map/jit(_where)/select_n | solution.py:21
  82.1 2.7 %pad_maximum_fusion = bf16[3,3,1024,256]{3,2,1,0:T(8,128)(2,1)} fusion(bf16[3,3,1024,128]{3,2,1,0:T(8,128)(2,1)S(1)} %get-tuple-element.6, bf16[3,3,1024,128]{3,2,1,0:T(8,128)(2,1)S(1)} %get-tuple-element.5), kind=kLoop, calls=%fused_computation.32 | loop fusion | flops 9437184 | bytes 9437184 | tf_op jit(solution)/shard_map/concatenate | solution.py:21
  84.8 18.8 %all-to-all-done.3 = bf16[32,56,256]{2,1,0:T(8,128)(2,1)S(1)} async-done(((bf16[32,56,256]{2,1,0:T(8,128)(2,1)}), bf16[32,56,256]{2,1,0:T(8,128)(2,1)S(1)}, u32[]{:S(2)}, u32[]{:S(2)}) %all-to-all-start.3) | async-done | bytes 917536 | tf_op jit(solution)/shard_map/all_to_all | solution.py:15
  103.6 0.7 pad_slice_fusion.1
  104.3 0.8 pad_slice_fusion
  105.1 0.0 slice-start
  105.6 0.0 slice-start.1
  106.2 1.0 slice-done
  107.3 0.2 slice-done.1
  107.5 2.3 %convolution_convert_fusion.1 = bf16[448,256]{1,0:T(8,128)(2,1)S(1)} fusion(bf16[448,9216]{1,0:T(8,128)(2,1)S(1)} %constant_dynamic-update-slice_fusion.45, bf16[9216,256]{1,0:T(8,128)(2,1)S(1)} %bitcast.113), kind=kOutput, calls=%fused_computation.36 | convolution fusion | flops 2114043904 | bytes 13205504 | tf_op jit(solution)/shard_map/dot_general | solution.py:72
  109.8 0.1 reshape.233
  109.9 23.9 %all_to_all.25 = bf16[16,56,128]{2,1,0:T(8,128)(2,1)S(1)} all-to-all(bf16[16,56,128]{2,1,0:T(8,128)(2,1)S(1)} %bitcast.118), channel_id=1, replica_groups=mesh['yl'=4,'core'=2,'x'=4,'yh'=2,'z'=8] {'core','x','yh'}, dimensions={0} | all-to-all | bytes 458752 | tf_op jit(solution)/shard_map/all_to_all | solution.py:15
  133.9 0.6 copy.30
  (97 shorter events, 2.0 us)
Async XLA Ops:
  0.0 2.5 %copy-start = (bf16[3,3,128,128]{3,2,1,0:T(8,128)(2,1)S(1)}, bf16[3,3,128,128]{3,2,1,0:T(8,128)(2,1)}, u32[]{:S(2)}) copy-start(bf16[3,3,128,128]{3,2,1,0:T(8,128)(2,1)} %param.5) | copy-start | bytes 884740
  0.0 12.3 %copy-start.1 = (bf16[3,3,128,128]{3,2,1,0:T(8,128)(2,1)S(1)}, bf16[3,3,128,128]{3,2,1,0:T(8,128)(2,1)}, u32[]{:S(2)}) copy-start(bf16[3,3,128,128]{3,2,1,0:T(8,128)(2,1)} %param.6) | copy-start | bytes 884740
  3.7 21.9 %all-to-all-start = ((bf16[8,112,128]{2,1,0:T(8,128)(2,1)}), bf16[8,112,128]{2,1,0:T(8,128)(2,1)S(1)}, u32[]{:S(2)}, u32[]{:S(2)}) async-start(bf16[8,112,128]{2,1,0:T(8,128)(2,1)} %bitcast.10), calls=%async_computation | async-start | bytes 458752 | tf_op jit(solution)/shard_map/all_to_all | solution.py:15
  12.3 19.4 %collective-permute-start = (bf16[3,3,128,128]{3,2,1,0:T(8,128)(2,1)S(1)}, bf16[3,3,128,128]{3,2,1,0:T(8,128)(2,1)S(1)}, u32[]{:S(2)}, u32[]{:S(2)}) collective-permute-start(bf16[3,3,128,128]{3,2,1,0:T(8,128)(2,1)S(1)} %copy-done.1), channel_id=1, source_target_pairs={{0,0},{1,64},{2,128},{3,192},{4,256},{5,320},{6,384},{7,448},{64,1... | collective-permute-start | bytes 884744 | tf_op jit(solution)/shard_map/ppermute | solution.py:92
  26.6 26.4 %all-to-all-start.1 = ((bf16[32,56,128]{2,1,0:T(8,128)(2,1)}), bf16[32,56,128]{2,1,0:T(8,128)(2,1)S(1)}, u32[]{:S(2)}, u32[]{:S(2)}) async-start(bf16[32,56,128]{2,1,0:T(8,128)(2,1)} %bitcast.13), calls=%async_computation.1 | async-start | bytes 917504 | tf_op jit(solution)/shard_map/all_to_all | solution.py:15
  31.8 6.6 %collective-permute-start.1 = (bf16[3,3,128,128]{3,2,1,0:T(8,128)(2,1)S(1)}, bf16[3,3,128,128]{3,2,1,0:T(8,128)(2,1)S(1)}, u32[]{:S(2)}, u32[]{:S(2)}) collective-permute-start(bf16[3,3,128,128]{3,2,1,0:T(8,128)(2,1)S(1)} %collective-permute-done), channel_id=1, source_target_pairs={{0,64},{64,0},{1,65},{65,1},{2,66},{66,2},{3,67},{67,3},{4,68},{68... | collective-permute-start | bytes 884744 | tf_op jit(solution)/shard_map/ppermute | solution.py:19
  36.4 43.0 %collective-permute-start.2 = (bf16[3,3,1024,128]{3,2,1,0:T(8,128)(2,1)}, bf16[3,3,1024,128]{3,2,1,0:T(8,128)(2,1)}, u32[]{:S(2)}, u32[]{:S(2)}) collective-permute-start(bf16[3,3,1024,128]{3,2,1,0:T(8,128)(2,1)} %param.7), channel_id=1, source_target_pairs={{0,64},{64,0},{1,65},{65,1},{2,66},{66,2},{3,67},{67,3},{4,68},{68... | collective-permute-start | bytes 7077896 | tf_op jit(solution)/shard_map/ppermute | solution.py:19
  54.8 17.3 %all-to-all-start.2 = ((bf16[8,56,256]{2,1,0:T(8,128)(2,1)}), bf16[8,56,256]{2,1,0:T(8,128)(2,1)S(1)}, u32[]{:S(2)}, u32[]{:S(2)}) async-start(bf16[8,56,256]{2,1,0:T(8,128)(2,1)} %bitcast.30), calls=%async_computation.2 | async-start | bytes 458752 | tf_op jit(solution)/shard_map/all_to_all | solution.py:15
  73.3 30.3 %all-to-all-start.3 = ((bf16[32,56,256]{2,1,0:T(8,128)(2,1)}), bf16[32,56,256]{2,1,0:T(8,128)(2,1)S(1)}, u32[]{:S(2)}, u32[]{:S(2)}) async-start(bf16[32,56,256]{2,1,0:T(8,128)(2,1)} %broadcast_in_dim.28), calls=%async_computation.3 | async-start | bytes 1835008 | tf_op jit(solution)/shard_map/all_to_all | solution.py:15
  105.1 2.2 %slice-start = ((s8[4718592]{0:T(1024)(128)(4,1)}), s8[4194304]{0:T(1024)(128)(4,1)S(1)}, s32[]{:S(2)}) async-start(s8[4718592]{0:T(1024)(128)(4,1)} %bitcast.111), calls=%async_computation.5 | async-start | bytes 8388608
  105.6 1.9 %slice-start.1 = ((s8[4718592]{0:T(1024)(128)(4,1)}), s8[524288]{0:T(1024)(128)(4,1)S(1)}, s32[]{:S(2)}) async-start(s8[4718592]{0:T(1024)(128)(4,1)} %bitcast.111), calls=%async_computation.6 | async-start | bytes 1048576

commit v2 on v1

v2 whole, which is shorter than its diff:
```python
import jax
import jax.numpy as jnp
from jax import lax
from jax.experimental import pallas as pl
from jax.experimental.pallas import tpu as pltpu
from jax.sharding import Mesh, PartitionSpec as P


YL, CORE, X, YH, Z = "yl", "core", "x", "yh", "z"
SIZES = (4, 2, 4, 2, 8)
SWAP = [(0, 1), (1, 0)]
BF = jnp.bfloat16
F32 = jnp.float32


def exchange(values, axes):
    return lax.all_to_all(values, axes, 0, 0, tiled=True)


def swap_cores(values):
    return lax.ppermute(values, CORE, SWAP)


def parity_planes(values):
    n, _, _, c = values.shape
    return values.reshape(n, 7, 2, 7, 2, c).transpose(2, 4, 0, 1, 3, 5).reshape(4, n, 7, 7, c)


def first_conv(part, weight):
    n, _, _, c = part.shape
    padded = jnp.pad(part, ((0, 0), (1, 1), (1, 1), (0, 0)))
    cells = padded.reshape(n, 8, 2, 8, 2, c).transpose(2, 4, 0, 1, 3, 5)
    cells = jnp.pad(cells, ((0, 0), (0, 0), (0, 0), (0, 0), (1, 0), (0, 0)))
    planes = []
    for row in range(2):
        for col in range(2):
            taps = []
            for a in range(3):
                for b in range(3):
                    i, qi = divmod(row + a, 2)
                    j, qj = divmod(col + b, 2)
                    taps.append(cells[qi, qj, :, i : i + 7, j : j + 8])
            planes.append(jnp.concatenate(taps, axis=3).reshape(n * 56, 9 * c))
    table = jnp.concatenate(planes, axis=0)
    return jnp.dot(table, weight.reshape(9 * c, -1), preferred_element_type=F32)


def reduce_kernel(place, planes, mine, theirs, out):
    yl, core = place[0], place[1]
    row = lax.broadcasted_iota(jnp.int32, (112, 128), 0)
    inner = lax.rem(row // 8, 7) > 0
    total = jnp.zeros((112, 128), F32)
    for kind, weight in ((core, mine), (1 - core, theirs)):
        for shift in range(4):
            block = lax.rem(yl + (4 - shift), 4) * 2 + kind
            taps = {}
            for p in range(2):
                for q in range(2):
                    value = jnp.concatenate([planes[2 * p + q, n, block].astype(F32) for n in range(2)], axis=0)
                    for b in (0, 2) if q else (1,):
                        moved = pltpu.roll(value, 1, 0) if b == 0 else value
                        for a in (0, 2) if p else (1,):
                            tap = jnp.where(inner, pltpu.roll(moved, 8, 0), 0.0) if a == 0 else moved
                            taps[a, b] = tap.astype(BF)
            table = jnp.concatenate([taps[a, b] for a in range(3) for b in range(3)], axis=1)
            total = total + jnp.dot(table, weight[shift], preferred_element_type=F32)
    out[...] = jnp.where(lax.rem(row, 8) > 0, jnp.maximum(total, 0.0), 0.0).astype(BF)


def reduce_conv(place, planes, mine, theirs):
    vmem = pl.BlockSpec(memory_space=pltpu.VMEM)
    return pl.pallas_call(
        reduce_kernel,
        out_shape=jax.ShapeDtypeStruct((112, 128), BF),
        in_specs=[pl.BlockSpec(memory_space=pltpu.SMEM), vmem, vmem, vmem],
        out_specs=vmem,
        name="reduce_conv",
    )(place, planes, mine, theirs)


def wide_table(maps):
    n, groups, _, _, c = maps.shape
    padded = jnp.pad(maps, ((0, 0), (0, 0), (1, 1), (1, 1), (0, 0)))
    taps = []
    for a in range(3):
        for b in range(3):
            for g in range(groups):
                taps.append(padded[:, g, a : a + 7, b : b + 8])
    return jnp.concatenate(taps, axis=3).reshape(n * 56, 9 * groups * c)


def real_columns(values):
    column = lax.broadcasted_iota(jnp.int32, values.shape, values.ndim - 2)
    return jnp.where(column > 0, values, jnp.zeros_like(values))


def all_inputs(w_reduce):
    blocks = [w_reduce.reshape(1152, 128)]
    for shift in range(1, 4):
        blocks.append(lax.ppermute(blocks[0], YL, [(j, (j + shift) % 4) for j in range(4)]))
    mine = jnp.stack(blocks)
    theirs = swap_cores(mine)
    return mine, theirs


def body(maps, w_first, w_reduce, w_wide):
    core = lax.axis_index(CORE)
    plane = lax.axis_index(X)
    in_block = lax.axis_index(X) * 2 + lax.axis_index(YH)
    out_block = lax.axis_index(Z)
    images = maps.reshape(2, 14, 14, 1024)
    part = lax.dynamic_slice_in_dim(images, in_block * 128, 128, 3)

    first = first_conv(jnp.maximum(part, 0), w_first).astype(BF).reshape(4, 1, 112, 128)
    first = exchange(jnp.broadcast_to(first, (4, 2, 112, 128)).reshape(8, 112, 128), (X, YH))
    summed = first.astype(F32).sum(0).reshape(2, 7, 8, 128)

    mine, theirs = all_inputs(w_reduce)
    other = swap_cores(w_wide)
    weight_wide = jnp.concatenate(
        [jnp.where(core == 0, w_wide, other), jnp.where(core == 0, other, w_wide)], axis=3
    ).reshape(9216, 256)

    own = lax.dynamic_slice_in_dim(images, out_block * 128, 128, 3)
    own = lax.dynamic_index_in_dim(parity_planes(own), plane, 0, keepdims=False)
    own = jnp.pad(own, ((0, 0), (0, 0), (1, 0), (0, 0)))
    segment = (own.astype(F32) + summed).astype(BF)
    segment = real_columns(jnp.maximum(segment, 0)).reshape(2, 1, 56, 128)

    spread = jnp.broadcast_to(segment, (2, 8, 56, 128)).reshape(16, 56, 128)
    chip = exchange(spread, (CORE, Z)).reshape(896, 128)
    spread = jnp.broadcast_to(chip, (4, 896, 128))
    planes = exchange(spread, (X,)).reshape(4, 2, 8, 56, 128)
    place = jnp.stack([lax.axis_index(YL), core]).astype(jnp.int32)
    narrow = reduce_conv(place, planes, mine, theirs)

    gathered = exchange(jnp.broadcast_to(narrow, (32, 112, 128)), (YL, Z))
    gathered = gathered.reshape(4, 8, 2, 7, 8, 128).transpose(0, 2, 1, 3, 4, 5).reshape(8, 8, 7, 8, 128)
    wide = jnp.dot(wide_table(gathered), weight_wide, preferred_element_type=F32).astype(BF)

    wide = wide.reshape(8, 56, 256)
    wide = jnp.concatenate([wide[..., :128], wide[..., 128:]], axis=0)
    wide = exchange(wide, (CORE, X, YH)).reshape(2, 8, 7, 8, 128)
    total = wide.astype(F32).sum(1).astype(BF)
    return total[:, None, :, 1:, :]


def solution(mesh):
    fine = Mesh(mesh.devices.reshape(SIZES), (YL, CORE, X, YH, Z))
    img, cin = (YL, CORE), (X, YH)
    in_specs = (
        P(None, img, None, None, None),
        P(None, None, cin, Z),
        P(None, None, img, cin + (Z,)),
        P(None, None, cin, img + (Z,)),
    )
    out_specs = P(None, cin, None, None, img + (Z,))
    return jax.shard_map(body, mesh=fine, in_specs=in_specs, out_specs=out_specs, check_vma=False)
```

time: 135 us -> 143 us (1.059)
  blocking collectives: 23.9 us -> 37.9 us
  waiting for transfers between devices: 52.3 us -> 44 us
  Pallas kernels: 0 us -> 3.31 us
  starting transfers between devices: 37.8 us -> 35 us
  local copies, waits for them, and re-layouts: 9.91 us -> 12 us
    all_to_all x4 -> x3, waiting for transfers between devices: 51.9 us -> 32.2 us  [exchange(): return lax.all_to_all(values, axes, 0, 0, tiled=True)]
    all_to_all x1 -> x2, blocking collectives: 23.9 us -> 37.9 us  [exchange(): return lax.all_to_all(values, axes, 0, 0, tiled=True)]
    ppermute x3 -> x5, waiting for transfers between devices: 0.4 us -> 11.8 us  [the longest x3 11.8 us: all_inputs(): lax.ppermute(blocks[0], YL, [(j, (j + shift) % 4) for j in range(4)])]
    all_to_all x4 -> x3, starting transfers between devices: 27.1 us -> 20.7 us  [exchange(): return lax.all_to_all(values, axes, 0, 0, tiled=True)]
    ppermute x3 -> x5, starting transfers between devices: 10.8 us -> 14.3 us  [the longest x3 10.5 us: all_inputs(): lax.ppermute(blocks[0], YL, [(j, (j + shift) % 4) for j in range(4)])]
    pallas_call x0 -> x1, Pallas kernels: none -> 3.31 us  [reduce_conv(): pl.pallas_call(reduce_kernel, out_shape=jax.ShapeDtypeStruct((112, 128),...]
    dot_general x2 -> x1, matrix products: 3.45 us -> 2.29 us  [body(): jnp.dot(wide_table(gathered), weight_wide, preferred_element_type=F32)]
    broadcast_in_dim x5 -> x6, local copies, waits for them, and re-layouts: 3.24 us -> 4.29 us  [the longest x1 1.82 us: body(): gathered = exchange(jnp.broadcast_to(narrow, (32, 112, 128)), (YL, Z))]
  transfers between devices with their start and end apart: 7 -> 8, of which waited for: 5 -> 5; matrix products, arithmetic and copies ran while one was open for 7% -> 9% of each run, Pallas kernels for 0% -> 2%
where the time goes in v2:
time: 143 us; the launch traced here: 142 us
  waiting for transfers between devices  44 us (31%)
  blocking collectives  37.9 us (27%)
  starting transfers between devices  35 us (24%)
  local copies, waits for them, and re-layouts  12 us (8%)
  other arithmetic  6.39 us (4%)
  Pallas kernels  3.31 us (2%)
  matrix products  2.73 us (2%)
    all_to_all x2, blocking collectives, exchange(): return lax.all_to_all(values, axes, 0, 0, tiled=True)  37.9 us
    all_to_all x3, waiting for transfers between devices, exchange(): return lax.all_to_all(values, axes, 0, 0, tiled=True)  32.2 us
    all_to_all x3, starting transfers between devices, exchange(): return lax.all_to_all(values, axes, 0, 0, tiled=True)  20.7 us
    ppermute x3, waiting for transfers between devices, all_inputs(): lax.ppermute(blocks[0], YL, [(j, (j + shift) % 4) for j in range(4)])  11.8 us
    ppermute x3, starting transfers between devices, all_inputs(): lax.ppermute(blocks[0], YL, [(j, (j + shift) % 4) for j in range(4)])  10.5 us
    ppermute x2, starting transfers between devices, swap_cores(): return lax.ppermute(values, CORE, SWAP)  3.84 us
    unnamed x110, local copies, waits for them, and re-layouts  3.72 us
    pallas_call x1, Pallas kernels, reduce_conv(): pl.pallas_call(reduce_kernel, out_shape=jax.ShapeDtypeStruct((112, 128),...  3.31 us
  transfers between devices with their start and end apart: 8, of which 5 were waited for; matrix products, arithmetic and copies ran while one was open for 9% of the time, Pallas kernels for 2%

profile of v2, /device:TPU:72, one launch (start us, length us, event | category | flops | bytes accessed | tf_op | source)
XLA Modules:
  0.0 142.5 jit_solution(12656253577738398038)
XLA Ops:
  0.0 0.0 copy-start
  0.0 3.6 %collective-permute-start = (bf16[1152,128]{1,0:T(8,128)(2,1)}, bf16[1152,128]{1,0:T(8,128)(2,1)S(1)}, u32[]{:S(2)}, u32[]{:S(2)}) collective-permute-start(bf16[1152,128]{1,0:T(8,128)(2,1)} %bitcast.216), channel_id=1, source_target_pairs={{0,128},{128,256},{256,384},{384,0},{1,129},{129,257},{257,385},{3... | collective-permute-start | bytes 884744 | tf_op jit(solution)/shard_map/ppermute | solution.py:100
  3.6 3.1 %collective-permute-start.1 = (bf16[1152,128]{1,0:T(8,128)(2,1)}, bf16[1152,128]{1,0:T(8,128)(2,1)S(1)}, u32[]{:S(2)}, u32[]{:S(2)}) collective-permute-start(bf16[1152,128]{1,0:T(8,128)(2,1)} %bitcast.217), channel_id=1, source_target_pairs={{0,256},{128,384},{256,0},{384,128},{1,257},{129,385},{257,1},{385... | collective-permute-start | bytes 884744 | tf_op jit(solution)/shard_map/ppermute | solution.py:100
  6.8 3.7 %collective-permute-start.2 = (bf16[1152,128]{1,0:T(8,128)(2,1)}, bf16[1152,128]{1,0:T(8,128)(2,1)S(1)}, u32[]{:S(2)}, u32[]{:S(2)}) collective-permute-start(bf16[1152,128]{1,0:T(8,128)(2,1)} %bitcast.218), channel_id=1, source_target_pairs={{0,384},{128,0},{256,128},{384,256},{1,385},{129,1},{257,129},{385... | collective-permute-start | bytes 884744 | tf_op jit(solution)/shard_map/ppermute | solution.py:100
  10.5 1.1 constant_dynamic-slice_fusion.1
  11.7 0.4 pad_slice_fusion.71
  12.1 0.2 fusion.12
  12.9 0.0 copy-done
  12.9 0.4 convolution_convert_fusion.1
  13.4 0.7 broadcast_in_dim.24
  14.1 7.8 %all-to-all-start = ((bf16[8,112,128]{2,1,0:T(8,128)(2,1)}), bf16[8,112,128]{2,1,0:T(8,128)(2,1)S(1)}, u32[]{:S(2)}, u32[]{:S(2)}) async-start(bf16[8,112,128]{2,1,0:T(8,128)(2,1)} %bitcast.12), calls=%async_computation | async-start | bytes 458752 | tf_op jit(solution)/shard_map/all_to_all | solution.py:17
  21.9 1.9 %collective-permute-start.4 = (bf16[3,3,1024,128]{3,2,1,0:T(8,128)(2,1)}, bf16[3,3,1024,128]{3,2,1,0:T(8,128)(2,1)}, u32[]{:S(2)}, u32[]{:S(2)}) collective-permute-start(bf16[3,3,1024,128]{3,2,1,0:T(8,128)(2,1)} %param.7), channel_id=1, source_target_pairs={{0,64},{64,0},{1,65},{65,1},{2,66},{66,2},{3,67},{67,3},{4,68},{68... | collective-permute-start | bytes 7077896 | tf_op jit(solution)/shard_map/ppermute | solution.py:21
  23.8 0.1 copy.24
  23.9 2.5 %collective-permute-done = bf16[1152,128]{1,0:T(8,128)(2,1)S(1)} collective-permute-done((bf16[1152,128]{1,0:T(8,128)(2,1)}, bf16[1152,128]{1,0:T(8,128)(2,1)S(1)}, u32[]{:S(2)}, u32[]{:S(2)}) %collective-permute-start) | collective-permute-done | bytes 294944 | tf_op jit(solution)/shard_map/ppermute | solution.py:100
  26.4 6.1 %collective-permute-done.1 = bf16[1152,128]{1,0:T(8,128)(2,1)S(1)} collective-permute-done((bf16[1152,128]{1,0:T(8,128)(2,1)}, bf16[1152,128]{1,0:T(8,128)(2,1)S(1)}, u32[]{:S(2)}, u32[]{:S(2)}) %collective-permute-start.1) | collective-permute-done | bytes 294944 | tf_op jit(solution)/shard_map/ppermute | solution.py:100
  32.6 3.2 %collective-permute-done.2 = bf16[1152,128]{1,0:T(8,128)(2,1)S(1)} collective-permute-done((bf16[1152,128]{1,0:T(8,128)(2,1)}, bf16[1152,128]{1,0:T(8,128)(2,1)S(1)}, u32[]{:S(2)}, u32[]{:S(2)}) %collective-permute-start.2) | collective-permute-done | bytes 294944 | tf_op jit(solution)/shard_map/ppermute | solution.py:100
  35.8 0.0 copy-done.3
  35.8 0.1 pad_maximum_fusion.1.mine
  35.9 0.0 copy-start.1
  35.9 1.9 %collective-permute-start.3 = (bf16[4,1152,128]{2,1,0:T(8,128)(2,1)S(1)}, bf16[4,1152,128]{2,1,0:T(8,128)(2,1)}, u32[]{:S(2)}, u32[]{:S(2)}) collective-permute-start(bf16[4,1152,128]{2,1,0:T(8,128)(2,1)S(1)} %pad_maximum_fusion.1.mine), channel_id=1, source_target_pairs={{0,64},{64,0},{1,65},{65,1},{2,66},{66,2},{3,67},{67,3},{4,68},{68... | collective-permute-start | bytes 3538952 | tf_op jit(solution)/shard_map/ppermute | solution.py:21
  37.9 0.0 all-to-all-done
  37.9 0.1 broadcast_select_fusion.2
  38.0 20.1 %all_to_all.25 = bf16[16,56,128]{2,1,0:T(8,128)(2,1)S(1)} all-to-all(bf16[16,56,128]{2,1,0:T(8,128)(2,1)S(1)} %bitcast.141), channel_id=1, replica_groups=mesh['yl'=4,'core'=2,'x'=4,'yh'=2,'z'=8] {'core','z'}, dimensions={0} | all-to-all | bytes 458752 | tf_op jit(solution)/shard_map/all_to_all | solution.py:17
  58.2 1.1 broadcast_in_dim.27
  59.3 4.3 %all-to-all-start.2 = ((bf16[4,896,128]{2,1,0:T(8,128)(2,1)}), bf16[4,896,128]{2,1,0:T(8,128)(2,1)S(1)}, u32[]{:S(2)}, u32[]{:S(2)}) async-start(bf16[4,896,128]{2,1,0:T(8,128)(2,1)} %broadcast_in_dim.27), calls=%async_computation.2 | async-start | bytes 1835008 | tf_op jit(solution)/shard_map/all_to_all | solution.py:17
  63.5 0.7 pad_add_fusion.place
  64.2 0.0 collective-permute-done.3.theirs
  64.2 12.1 %all-to-all-done.2 = bf16[4,896,128]{2,1,0:T(8,128)(2,1)S(1)} async-done(((bf16[4,896,128]{2,1,0:T(8,128)(2,1)}), bf16[4,896,128]{2,1,0:T(8,128)(2,1)S(1)}, u32[]{:S(2)}, u32[]{:S(2)}) %all-to-all-start.2) | async-done | bytes 917536 | tf_op jit(solution)/shard_map/all_to_all | solution.py:17
  76.3 0.9 copy-done.2
  77.3 3.3 %reduce_conv.1 = bf16[112,128]{1,0:T(8,128)(2,1)} custom-call(s32[2]{0:T(128)} %pad_add_fusion.place, bf16[4,2,8,56,128]{4,3,2,1,0:T(8,128)(2,1)} %bitcast.139, bf16[4,1152,128]{2,1,0:T(8,128)(2,1)} %copy-done.1, bf16[4,1152,128]{2,1,0:T(8,128)(2,1)} %collective-permute-done.3.theirs), custom_call_target="tpu_custom_call" | custom-call | tf_op jit(solution)/shard_map/reduce_conv/pallas_call | solution.py:72
  80.6 1.8 %broadcast_in_dim.28 = bf16[32,112,128]{2,1,0:T(8,128)(2,1)} broadcast(bf16[112,128]{1,0:T(8,128)(2,1)} %reduce_conv.1), dimensions={1,2} | broadcast | bytes 946176 | tf_op jit(solution)/shard_map/broadcast_in_dim | solution.py:137
  82.4 8.6 %all-to-all-start.3 = ((bf16[32,112,128]{2,1,0:T(8,128)(2,1)}), bf16[32,112,128]{2,1,0:T(8,128)(2,1)S(1)}, u32[]{:S(2)}, u32[]{:S(2)}) async-start(bf16[32,112,128]{2,1,0:T(8,128)(2,1)} %broadcast_in_dim.28), calls=%async_computation.3 | async-start | bytes 1835008 | tf_op jit(solution)/shard_map/all_to_all | solution.py:17
  91.0 0.0 collective-permute-done.4
  91.0 2.7 %broadcast_select_fusion.1 = (bf16[3,3,1024,128]{3,2,1,0:T(8,128)(2,1)S(1)}, bf16[3,3,1024,128]{3,2,1,0:T(8,128)(2,1)S(1)}) fusion(bf16[3,3,1024,128]{3,2,1,0:T(8,128)(2,1)} %param.7, bf16[3,3,1024,128]{3,2,1,0:T(8,128)(2,1)} %collective-permute-done.4, pred[]{:T(512)S(6)} %eq.4), kind=kLoop, calls=%fused_computation.66 | loop fusion | flops 2359296 | bytes 9437185 | tf_op jit(solution)/shard_map/jit(_where)/select_n | solution.py:121
  93.7 2.7 %pad_maximum_fusion = bf16[3,3,1024,256]{3,2,1,0:T(8,128)(2,1)} fusion(bf16[3,3,1024,128]{3,2,1,0:T(8,128)(2,1)S(1)} %get-tuple-element.6, bf16[3,3,1024,128]{3,2,1,0:T(8,128)(2,1)S(1)} %get-tuple-element.5), kind=kLoop, calls=%fused_computation.64 | loop fusion | flops 9437184 | bytes 9437184 | tf_op jit(solution)/shard_map/concatenate | solution.py:120
  96.4 20.1 %all-to-all-done.3 = bf16[32,112,128]{2,1,0:T(8,128)(2,1)S(1)} async-done(((bf16[32,112,128]{2,1,0:T(8,128)(2,1)}), bf16[32,112,128]{2,1,0:T(8,128)(2,1)S(1)}, u32[]{:S(2)}, u32[]{:S(2)}) %all-to-all-start.3) | async-done | bytes 917536 | tf_op jit(solution)/shard_map/all_to_all | solution.py:17
  116.5 0.1 copy.28
  116.6 0.3 pad_slice_fusion.3
  116.9 0.4 pad_slice_fusion
  117.4 0.7 pad_slice_fusion.1
  118.1 0.5 pad_slice_fusion.2
  118.6 0.0 slice-start
  120.1 0.0 slice-start.1
  121.6 0.0 slice-done
  121.6 0.0 slice-done.1
  121.6 2.3 %convolution_convert_fusion = bf16[448,256]{1,0:T(8,128)(2,1)S(1)} fusion(bf16[448,9216]{1,0:T(8,128)(2,1)S(1)} %constant_dynamic-update-slice_fusion.36, bf16[9216,256]{1,0:T(8,128)(2,1)S(1)} %bitcast.135), kind=kOutput, calls=%fused_computation.67 | convolution fusion | flops 2114043904 | bytes 13205504 | tf_op jit(solution)/shard_map/dot_general | solution.py:139
  124.0 17.8 %all_to_all.26 = bf16[16,56,128]{2,1,0:T(8,128)(2,1)S(1)} all-to-all(bf16[16,56,128]{2,1,0:T(8,128)(2,1)S(1)} %pad_maximum_fusion.2), channel_id=1, replica_groups=mesh['yl'=4,'core'=2,'x'=4,'yh'=2,'z'=8] {'core','x','yh'}, dimensions={0} | all-to-all | bytes 458752 | tf_op jit(solution)/shard_map/all_to_all | solution.py:17
  141.8 0.6 copy.29
  (118 shorter events, 3.2 us)
Async XLA Ops:
  0.0 12.9 %copy-start = (bf16[3,3,128,128]{3,2,1,0:T(8,128)(2,1)S(1)}, bf16[3,3,128,128]{3,2,1,0:T(8,128)(2,1)}, u32[]{:S(2)}) copy-start(bf16[3,3,128,128]{3,2,1,0:T(8,128)(2,1)} %param.5) | copy-start | bytes 884740
  0.0 35.7 %copy-start.3 = (bf16[3,3,128,128]{3,2,1,0:T(8,128)(2,1)S(1)}, bf16[3,3,128,128]{3,2,1,0:T(8,128)(2,1)}, u32[]{:S(2)}) copy-start(bf16[3,3,128,128]{3,2,1,0:T(8,128)(2,1)} %param.6) | copy-start | bytes 884740
  0.0 26.4 %collective-permute-start = (bf16[1152,128]{1,0:T(8,128)(2,1)}, bf16[1152,128]{1,0:T(8,128)(2,1)S(1)}, u32[]{:S(2)}, u32[]{:S(2)}) collective-permute-start(bf16[1152,128]{1,0:T(8,128)(2,1)} %bitcast.216), channel_id=1, source_target_pairs={{0,128},{128,256},{256,384},{384,0},{1,129},{129,257},{257,385},{3... | collective-permute-start | bytes 884744 | tf_op jit(solution)/shard_map/ppermute | solution.py:100
  3.6 29.0 %collective-permute-start.1 = (bf16[1152,128]{1,0:T(8,128)(2,1)}, bf16[1152,128]{1,0:T(8,128)(2,1)S(1)}, u32[]{:S(2)}, u32[]{:S(2)}) collective-permute-start(bf16[1152,128]{1,0:T(8,128)(2,1)} %bitcast.217), channel_id=1, source_target_pairs={{0,256},{128,384},{256,0},{384,128},{1,257},{129,385},{257,1},{385... | collective-permute-start | bytes 884744 | tf_op jit(solution)/shard_map/ppermute | solution.py:100
  6.8 29.0 %collective-permute-start.2 = (bf16[1152,128]{1,0:T(8,128)(2,1)}, bf16[1152,128]{1,0:T(8,128)(2,1)S(1)}, u32[]{:S(2)}, u32[]{:S(2)}) collective-permute-start(bf16[1152,128]{1,0:T(8,128)(2,1)} %bitcast.218), channel_id=1, source_target_pairs={{0,384},{128,0},{256,128},{384,256},{1,385},{129,1},{257,129},{385... | collective-permute-start | bytes 884744 | tf_op jit(solution)/shard_map/ppermute | solution.py:100
  14.1 23.7 %all-to-all-start = ((bf16[8,112,128]{2,1,0:T(8,128)(2,1)}), bf16[8,112,128]{2,1,0:T(8,128)(2,1)S(1)}, u32[]{:S(2)}, u32[]{:S(2)}) async-start(bf16[8,112,128]{2,1,0:T(8,128)(2,1)} %bitcast.12), calls=%async_computation | async-start | bytes 458752 | tf_op jit(solution)/shard_map/all_to_all | solution.py:17
  21.9 69.1 %collective-permute-start.4 = (bf16[3,3,1024,128]{3,2,1,0:T(8,128)(2,1)}, bf16[3,3,1024,128]{3,2,1,0:T(8,128)(2,1)}, u32[]{:S(2)}, u32[]{:S(2)}) collective-permute-start(bf16[3,3,1024,128]{3,2,1,0:T(8,128)(2,1)} %param.7), channel_id=1, source_target_pairs={{0,64},{64,0},{1,65},{65,1},{2,66},{66,2},{3,67},{67,3},{4,68},{68... | collective-permute-start | bytes 7077896 | tf_op jit(solution)/shard_map/ppermute | solution.py:21
  35.9 40.4 %copy-start.1 = (bf16[4,1152,128]{2,1,0:T(8,128)(2,1)}, bf16[4,1152,128]{2,1,0:T(8,128)(2,1)S(1)}, u32[]{:S(2)}) copy-start(bf16[4,1152,128]{2,1,0:T(8,128)(2,1)S(1)} %pad_maximum_fusion.1.mine) | copy-start | bytes 3538948
  35.9 28.3 %collective-permute-start.3 = (bf16[4,1152,128]{2,1,0:T(8,128)(2,1)S(1)}, bf16[4,1152,128]{2,1,0:T(8,128)(2,1)}, u32[]{:S(2)}, u32[]{:S(2)}) collective-permute-start(bf16[4,1152,128]{2,1,0:T(8,128)(2,1)S(1)} %pad_maximum_fusion.1.mine), channel_id=1, source_target_pairs={{0,64},{64,0},{1,65},{65,1},{2,66},{66,2},{3,67},{67,3},{4,68},{68... | collective-permute-start | bytes 3538952 | tf_op jit(solution)/shard_map/ppermute | solution.py:21
  59.3 17.1 %all-to-all-start.2 = ((bf16[4,896,128]{2,1,0:T(8,128)(2,1)}), bf16[4,896,128]{2,1,0:T(8,128)(2,1)S(1)}, u32[]{:S(2)}, u32[]{:S(2)}) async-start(bf16[4,896,128]{2,1,0:T(8,128)(2,1)} %broadcast_in_dim.27), calls=%async_computation.2 | async-start | bytes 1835008 | tf_op jit(solution)/shard_map/all_to_all | solution.py:17
  76.3 1.0 copy-start.2
  82.4 34.1 %all-to-all-start.3 = ((bf16[32,112,128]{2,1,0:T(8,128)(2,1)}), bf16[32,112,128]{2,1,0:T(8,128)(2,1)S(1)}, u32[]{:S(2)}, u32[]{:S(2)}) async-start(bf16[32,112,128]{2,1,0:T(8,128)(2,1)} %broadcast_in_dim.28), calls=%async_computation.3 | async-start | bytes 1835008 | tf_op jit(solution)/shard_map/all_to_all | solution.py:17
  118.6 3.0 %slice-start = ((s8[4718592]{0:T(1024)(128)(4,1)}), s8[4194304]{0:T(1024)(128)(4,1)S(1)}, s32[]{:S(2)}) async-start(s8[4718592]{0:T(1024)(128)(4,1)} %bitcast.133), calls=%async_computation.5 | async-start | bytes 8388608
  120.1 1.5 %slice-start.1 = ((s8[4718592]{0:T(1024)(128)(4,1)}), s8[524288]{0:T(1024)(128)(4,1)S(1)}, s32[]{:S(2)}) async-start(s8[4718592]{0:T(1024)(128)(4,1)} %bitcast.133), calls=%async_computation.6 | async-start | bytes 1048576

commit v3 on v2

--- a/solution.py
+++ b/solution.py
@@ -45,48 +45,122 @@
     return jnp.dot(table, weight.reshape(9 * c, -1), preferred_element_type=F32)
 
 
-def reduce_kernel(place, planes, mine, theirs, out):
+def nine_taps(value, rows, inner_top, inner_bottom):
+    count = value.shape[0]
+    taps = []
+    for a in range(3):
+        for b in range(3):
+            moved = value if b == 1 else rows[b]
+            if a == 0:
+                moved = jnp.where(inner_top, pltpu.roll(moved, 8, 0), 0.0)
+            elif a == 2:
+                moved = jnp.where(inner_bottom, pltpu.roll(moved, count - 8, 0), 0.0)
+            taps.append(moved.astype(BF))
+    return jnp.concatenate(taps, axis=1)
+
+
+def reduce_kernel(place, planes, mine, theirs, out, planes_v, mine_v, theirs_v, narrow, sems, out_sems):
     yl, core = place[0], place[1]
+    copies = []
+    for kind, source, held in ((0, mine, mine_v), (1, theirs, theirs_v)):
+        own = core if kind == 0 else 1 - core
+        for shift in range(4):
+            step = 4 * kind + shift
+            block = lax.rem(yl + (4 - shift), 4) * 2 + own
+            pair = (
+                pltpu.make_async_copy(planes.at[:, :, block], planes_v.at[step], sems.at[0, step]),
+                pltpu.make_async_copy(source.at[shift], held.at[shift], sems.at[1, step]),
+            )
+            for copy in pair:
+                copy.start()
+            copies.append(pair)
     row = lax.broadcasted_iota(jnp.int32, (112, 128), 0)
     inner = lax.rem(row // 8, 7) > 0
     total = jnp.zeros((112, 128), F32)
-    for kind, weight in ((core, mine), (1 - core, theirs)):
-        for shift in range(4):
-            block = lax.rem(yl + (4 - shift), 4) * 2 + kind
-            taps = {}
-            for p in range(2):
-                for q in range(2):
-                    value = jnp.concatenate([planes[2 * p + q, n, block].astype(F32) for n in range(2)], axis=0)
-                    for b in (0, 2) if q else (1,):
-                        moved = pltpu.roll(value, 1, 0) if b == 0 else value
-                        for a in (0, 2) if p else (1,):
-                            tap = jnp.where(inner, pltpu.roll(moved, 8, 0), 0.0) if a == 0 else moved
-                            taps[a, b] = tap.astype(BF)
-            table = jnp.concatenate([taps[a, b] for a in range(3) for b in range(3)], axis=1)
-            total = total + jnp.dot(table, weight[shift], preferred_element_type=F32)
-    out[...] = jnp.where(lax.rem(row, 8) > 0, jnp.maximum(total, 0.0), 0.0).astype(BF)
+    for step in range(8):
+        for copy in copies[step]:
+            copy.wait()
+        taps = {}
+        for p in range(2):
+            for q in range(2):
+                value = jnp.concatenate([planes_v[step, 2 * p + q, n].astype(F32) for n in range(2)], axis=0)
+                for b in (0, 2) if q else (1,):
+                    moved = pltpu.roll(value, 1, 0) if b == 0 else value
+                    for a in (0, 2) if p else (1,):
+                        tap = jnp.where(inner, pltpu.roll(moved, 8, 0), 0.0) if a == 0 else moved
+                        taps[a, b] = tap.astype(BF)
+        table = jnp.concatenate([taps[a, b] for a in range(3) for b in range(3)], axis=1)
+        weight = (mine_v if step < 4 else theirs_v)[step % 4]
+        total = total + jnp.dot(table, weight, preferred_element_type=F32)
+    narrow[...] = jnp.where(lax.rem(row, 8) > 0, jnp.maximum(total, 0.0), 0.0).astype(BF)
+    sent = [pltpu.make_async_copy(narrow, out.at[n], out_sems.at[n]) for n in range(32)]
+    for copy in sent:
+        copy.start()
+    for copy in sent:
+        copy.wait()
 
 
 def reduce_conv(place, planes, mine, theirs):
-    vmem = pl.BlockSpec(memory_space=pltpu.VMEM)
+    hbm = pl.BlockSpec(memory_space=pl.ANY)
     return pl.pallas_call(
         reduce_kernel,
-        out_shape=jax.ShapeDtypeStruct((112, 128), BF),
-        in_specs=[pl.BlockSpec(memory_space=pltpu.SMEM), vmem, vmem, vmem],
-        out_specs=vmem,
+        out_shape=jax.ShapeDtypeStruct((32, 112, 128), BF),
+        in_specs=[pl.BlockSpec(memory_space=pltpu.SMEM), hbm, hbm, hbm],
+        out_specs=hbm,
+        scratch_shapes=[
+            pltpu.VMEM((8, 4, 2, 56, 128), BF),
+            pltpu.VMEM((4, 1152, 128), BF),
+            pltpu.VMEM((4, 1152, 128), BF),
+            pltpu.VMEM((112, 128), BF),
+            pltpu.SemaphoreType.DMA((2, 8)),
+            pltpu.SemaphoreType.DMA((32,)),
+        ],
         name="reduce_conv",
     )(place, planes, mine, theirs)
 
 
-def wide_table(maps):
-    n, groups, _, _, c = maps.shape
-    padded = jnp.pad(maps, ((0, 0), (0, 0), (1, 1), (1, 1), (0, 0)))
-    taps = []
-    for a in range(3):
-        for b in range(3):
-            for g in range(groups):
-                taps.append(padded[:, g, a : a + 7, b : b + 8])
-    return jnp.concatenate(taps, axis=3).reshape(n * 56, 9 * groups * c)
+def wide_kernel(place, maps, own, other, out, maps_v, own_v, other_v, sems):
+    core = place[1]
+    copies = []
+    for z in range(8):
+        channels = pl.ds(128 * z, 128)
+        trio = (
+            pltpu.make_async_copy(maps.at[:, z], maps_v.at[z], sems.at[0, z]),
+            pltpu.make_async_copy(own.at[:, channels], own_v.at[z], sems.at[1, z]),
+            pltpu.make_async_copy(other.at[:, channels], other_v.at[z], sems.at[2, z]),
+        )
+        for copy in trio:
+            copy.start()
+        copies.append(trio)
+    line = lax.rem(lax.broadcasted_iota(jnp.int32, (448, 128), 0) // 8, 7)
+    total = jnp.zeros((448, 256), F32)
+    for z in range(8):
+        for copy in copies[z]:
+            copy.wait()
+        value = maps_v[z].reshape(448, 128).astype(F32)
+        rows = {0: pltpu.roll(value, 1, 0), 2: pltpu.roll(value, 447, 0)}
+        table = nine_taps(value, rows, line > 0, line < 6)
+        weight = jnp.concatenate([own_v[z].reshape(1152, 128), other_v[z].reshape(1152, 128)], axis=1)
+        total = total + jnp.dot(table, weight, preferred_element_type=F32)
+    out[core] = total[:, :128].astype(BF).reshape(8, 56, 128)
+    out[1 - core] = total[:, 128:].astype(BF).reshape(8, 56, 128)
+
+
+def wide_conv(place, maps, own, other):
+    hbm = pl.BlockSpec(memory_space=pl.ANY)
+    return pl.pallas_call(
+        wide_kernel,
+        out_shape=jax.ShapeDtypeStruct((2, 8, 56, 128), BF),
+        in_specs=[pl.BlockSpec(memory_space=pltpu.SMEM), hbm, hbm, hbm],
+        out_specs=pl.BlockSpec(memory_space=pltpu.VMEM),
+        scratch_shapes=[
+            pltpu.VMEM((8, 4, 112, 128), BF),
+            pltpu.VMEM((8, 9, 128, 128), BF),
+            pltpu.VMEM((8, 9, 128, 128), BF),
+            pltpu.SemaphoreType.DMA((3, 8)),
+        ],
+        name="wide_conv",
+    )(place, maps, own, other)
 
 
 def real_columns(values):
@@ -117,9 +191,6 @@
 
     mine, theirs = all_inputs(w_reduce)
     other = swap_cores(w_wide)
-    weight_wide = jnp.concatenate(
-        [jnp.where(core == 0, w_wide, other), jnp.where(core == 0, other, w_wide)], axis=3
-    ).reshape(9216, 256)
 
     own = lax.dynamic_slice_in_dim(images, out_block * 128, 128, 3)
     own = lax.dynamic_index_in_dim(parity_planes(own), plane, 0, keepdims=False)
@@ -134,12 +205,10 @@
     place = jnp.stack([lax.axis_index(YL), core]).astype(jnp.int32)
     narrow = reduce_conv(place, planes, mine, theirs)
 
-    gathered = exchange(jnp.broadcast_to(narrow, (32, 112, 128)), (YL, Z))
-    gathered = gathered.reshape(4, 8, 2, 7, 8, 128).transpose(0, 2, 1, 3, 4, 5).reshape(8, 8, 7, 8, 128)
-    wide = jnp.dot(wide_table(gathered), weight_wide, preferred_element_type=F32).astype(BF)
-
-    wide = wide.reshape(8, 56, 256)
-    wide = jnp.concatenate([wide[..., :128], wide[..., 128:]], axis=0)
+    gathered = exchange(narrow, (YL, Z)).reshape(4, 8, 112, 128)
+    wide = wide_conv(place, gathered, w_wide.reshape(9, 1024, 128), other.reshape(9, 1024, 128))
+
+    wide = wide.reshape(16, 56, 128)
     wide = exchange(wide, (CORE, X, YH)).reshape(2, 8, 7, 8, 128)
     total = wide.astype(F32).sum(1).astype(BF)
     return total[:, None, :, 1:, :]

time: 143 us -> 144 us (level)
  Pallas kernels: 3.31 us -> 12.8 us
  waiting for transfers between devices: 44 us -> 52.8 us
  other arithmetic: 6.39 us -> 0.94 us
  local copies, waits for them, and re-layouts: 12 us -> 6.65 us
  starting transfers between devices: 35 us -> 31.3 us
  matrix products: 2.73 us -> 0.44 us
    pallas_call x1 -> x2, Pallas kernels: 3.31 us -> 12.8 us  [the longest x1 7.91 us: wide_conv(): pl.pallas_call(wide_kernel, out_shape=jax.ShapeDtypeStruct((2, 8, 56, 128...]
    all_to_all x3, waiting for transfers between devices: 32.2 us -> 38.8 us  [exchange(): return lax.all_to_all(values, axes, 0, 0, tiled=True)]
    all_to_all x3, starting transfers between devices: 20.7 us -> 16.1 us  [exchange(): return lax.all_to_all(values, axes, 0, 0, tiled=True)]
    concatenate x2 -> x0, other arithmetic: 2.72 us -> none  [the longest x1 2.7 us: body(): jnp.concatenate([jnp.where(core == 0, w_wide, other), jnp.where(core == 0...]
    select_n x1 -> x0, other arithmetic: 2.69 us -> none  [body(): jnp.where(core == 0, w_wide, other)]
    dot_general x1 -> x0, matrix products: 2.29 us -> none  [body(): jnp.dot(wide_table(gathered), weight_wide, preferred_element_type=F32)]
    ppermute x3, waiting for transfers between devices: 11.8 us -> 14 us  [all_inputs(): lax.ppermute(blocks[0], YL, [(j, (j + shift) % 4) for j in range(4)])]
    slice x5 -> x0, local copies, waits for them, and re-layouts: 1.94 us -> none  [the longest x4 1.9 us: wide_table(): taps.append(padded[:, g, a:a + 7, b:b + 8])]
  transfers between devices with their start and end apart: 8 -> 8, of which waited for: 5 -> 5; matrix products, arithmetic and copies ran while one was open for 9% -> 4% of each run, Pallas kernels for 2% -> 3%
where the time goes in v3:
time: 144 us; the launch traced here: 143 us
  waiting for transfers between devices  52.8 us (37%)
  blocking collectives  37.9 us (26%)
  starting transfers between devices  31.3 us (22%)
  Pallas kernels  12.8 us (9%)
  local copies, waits for them, and re-layouts  6.65 us (5%)
    all_to_all x3, waiting for transfers between devices, exchange(): return lax.all_to_all(values, axes, 0, 0, tiled=True)  38.8 us
    all_to_all x2, blocking collectives, exchange(): return lax.all_to_all(values, axes, 0, 0, tiled=True)  37.9 us
    all_to_all x3, starting transfers between devices, exchange(): return lax.all_to_all(values, axes, 0, 0, tiled=True)  16.1 us
    ppermute x3, waiting for transfers between devices, all_inputs(): lax.ppermute(blocks[0], YL, [(j, (j + shift) % 4) for j in range(4)])  14 us
    ppermute x3, starting transfers between devices, all_inputs(): lax.ppermute(blocks[0], YL, [(j, (j + shift) % 4) for j in range(4)])  11.4 us
    pallas_call x1, Pallas kernels, wide_conv(): pl.pallas_call(wide_kernel, out_shape=jax.ShapeDtypeStruct((2, 8, 56, 128...  7.91 us
    pallas_call x1, Pallas kernels, reduce_conv(): pl.pallas_call(reduce_kernel, out_shape=jax.ShapeDtypeStruct((32, 112, 12...  4.88 us
    ppermute x2, starting transfers between devices, swap_cores(): return lax.ppermute(values, CORE, SWAP)  3.85 us
  transfers between devices with their start and end apart: 8, of which 5 were waited for; matrix products, arithmetic and copies ran while one was open for 4% of the time, Pallas kernels for 3%

profile of v3, /device:TPU:72, one launch (start us, length us, event | category | flops | bytes accessed | tf_op | source)
XLA Modules:
  0.0 143.3 jit_solution(18102064935032243601)
XLA Ops:
  0.0 0.0 copy-start
  0.0 2.5 %collective-permute-start.2 = (bf16[1152,128]{1,0:T(8,128)(2,1)}, bf16[1152,128]{1,0:T(8,128)(2,1)S(1)}, u32[]{:S(2)}, u32[]{:S(2)}) collective-permute-start(bf16[1152,128]{1,0:T(8,128)(2,1)} %bitcast.63), channel_id=1, source_target_pairs={{0,384},{128,0},{256,128},{384,256},{1,385},{129,1},{257,129},{385... | collective-permute-start | bytes 884744 | tf_op jit(solution)/shard_map/ppermute | solution.py:174
  2.5 4.5 %collective-permute-start.1 = (bf16[1152,128]{1,0:T(8,128)(2,1)}, bf16[1152,128]{1,0:T(8,128)(2,1)S(1)}, u32[]{:S(2)}, u32[]{:S(2)}) collective-permute-start(bf16[1152,128]{1,0:T(8,128)(2,1)} %bitcast.64), channel_id=1, source_target_pairs={{0,256},{128,384},{256,0},{384,128},{1,257},{129,385},{257,1},{385... | collective-permute-start | bytes 884744 | tf_op jit(solution)/shard_map/ppermute | solution.py:174
  7.0 4.4 %collective-permute-start = (bf16[1152,128]{1,0:T(8,128)(2,1)}, bf16[1152,128]{1,0:T(8,128)(2,1)S(1)}, u32[]{:S(2)}, u32[]{:S(2)}) collective-permute-start(bf16[1152,128]{1,0:T(8,128)(2,1)} %bitcast.65), channel_id=1, source_target_pairs={{0,128},{128,256},{256,384},{384,0},{1,129},{129,257},{257,385},{3... | collective-permute-start | bytes 884744 | tf_op jit(solution)/shard_map/ppermute | solution.py:174
  11.4 1.1 constant_dynamic-slice_fusion.1
  12.6 0.2 fusion.11
  12.8 0.4 pad_slice_fusion.7
  13.8 0.0 copy-done
  13.8 0.0 copy-start.4
  13.9 0.4 convolution_convert_fusion
  14.3 0.7 broadcast_in_dim.21
  15.0 6.9 %all-to-all-start = ((bf16[8,112,128]{2,1,0:T(8,128)(2,1)}), bf16[8,112,128]{2,1,0:T(8,128)(2,1)S(1)}, u32[]{:S(2)}, u32[]{:S(2)}) async-start(bf16[8,112,128]{2,1,0:T(8,128)(2,1)} %bitcast.12), calls=%async_computation | async-start | bytes 458752 | tf_op jit(solution)/shard_map/all_to_all | solution.py:17
  21.9 0.1 copy.20
  22.0 5.2 %collective-permute-done.2 = bf16[1152,128]{1,0:T(8,128)(2,1)S(1)} collective-permute-done((bf16[1152,128]{1,0:T(8,128)(2,1)}, bf16[1152,128]{1,0:T(8,128)(2,1)S(1)}, u32[]{:S(2)}, u32[]{:S(2)}) %collective-permute-start.2) | collective-permute-done | bytes 294944 | tf_op jit(solution)/shard_map/ppermute | solution.py:174
  27.2 0.0 collective-permute-done.1
  27.2 8.8 %collective-permute-done = bf16[1152,128]{1,0:T(8,128)(2,1)S(1)} collective-permute-done((bf16[1152,128]{1,0:T(8,128)(2,1)}, bf16[1152,128]{1,0:T(8,128)(2,1)S(1)}, u32[]{:S(2)}, u32[]{:S(2)}) %collective-permute-start) | collective-permute-done | bytes 294944 | tf_op jit(solution)/shard_map/ppermute | solution.py:174
  36.0 0.0 copy-done.4
  36.0 0.1 pad_maximum_fusion.mine
  36.2 0.0 copy-start.1
  36.2 1.9 %collective-permute-start.3 = (bf16[4,1152,128]{2,1,0:T(8,128)(2,1)S(1)}, bf16[4,1152,128]{2,1,0:T(8,128)(2,1)}, u32[]{:S(2)}, u32[]{:S(2)}) collective-permute-start(bf16[4,1152,128]{2,1,0:T(8,128)(2,1)S(1)} %pad_maximum_fusion.mine), channel_id=1, source_target_pairs={{0,64},{64,0},{1,65},{65,1},{2,66},{66,2},{3,67},{67,3},{4,68},{68... | collective-permute-start | bytes 3538952 | tf_op jit(solution)/shard_map/ppermute | solution.py:21
  38.1 2.8 %all-to-all-done = bf16[8,112,128]{2,1,0:T(8,128)(2,1)S(1)} async-done(((bf16[8,112,128]{2,1,0:T(8,128)(2,1)}), bf16[8,112,128]{2,1,0:T(8,128)(2,1)S(1)}, u32[]{:S(2)}, u32[]{:S(2)}) %all-to-all-start) | async-done | bytes 229408 | tf_op jit(solution)/shard_map/all_to_all | solution.py:17
  41.0 0.1 broadcast_select_fusion
  41.1 20.0 %all_to_all.25 = bf16[16,56,128]{2,1,0:T(8,128)(2,1)S(1)} all-to-all(bf16[16,56,128]{2,1,0:T(8,128)(2,1)S(1)} %bitcast.59), channel_id=1, replica_groups=mesh['yl'=4,'core'=2,'x'=4,'yh'=2,'z'=8] {'core','z'}, dimensions={0} | all-to-all | bytes 458752 | tf_op jit(solution)/shard_map/all_to_all | solution.py:17
  61.2 1.1 broadcast_in_dim.24
  62.2 0.0 copy-done.1
  62.2 3.5 %all-to-all-start.2 = ((bf16[4,896,128]{2,1,0:T(8,128)(2,1)}), bf16[4,896,128]{2,1,0:T(8,128)(2,1)S(1)}, u32[]{:S(2)}, u32[]{:S(2)}) async-start(bf16[4,896,128]{2,1,0:T(8,128)(2,1)} %broadcast_in_dim.24), calls=%async_computation.2 | async-start | bytes 1835008 | tf_op jit(solution)/shard_map/all_to_all | solution.py:17
  65.8 1.9 %collective-permute-start.4 = (bf16[3,3,1024,128]{3,2,1,0:T(8,128)(2,1)}, bf16[3,3,1024,128]{3,2,1,0:T(8,128)(2,1)}, u32[]{:S(2)}, u32[]{:S(2)}) collective-permute-start(bf16[3,3,1024,128]{3,2,1,0:T(8,128)(2,1)} %param.7), channel_id=1, source_target_pairs={{0,64},{64,0},{1,65},{65,1},{2,66},{66,2},{3,67},{67,3},{4,68},{68... | collective-permute-start | bytes 7077896 | tf_op jit(solution)/shard_map/ppermute | solution.py:21
  67.7 0.6 pad_add_fusion.place
  68.3 0.0 collective-permute-done.3.theirs
  68.3 10.5 %all-to-all-done.2 = bf16[4,896,128]{2,1,0:T(8,128)(2,1)S(1)} async-done(((bf16[4,896,128]{2,1,0:T(8,128)(2,1)}), bf16[4,896,128]{2,1,0:T(8,128)(2,1)S(1)}, u32[]{:S(2)}, u32[]{:S(2)}) %all-to-all-start.2) | async-done | bytes 917536 | tf_op jit(solution)/shard_map/all_to_all | solution.py:17
  78.8 0.0 copy-start.2
  78.8 1.0 copy-done.2
  79.7 4.9 %reduce_conv.1 = bf16[32,112,128]{2,1,0:T(8,128)(2,1)} custom-call(s32[2]{0:T(128)} %pad_add_fusion.place, bf16[4,2,8,56,128]{4,3,2,1,0:T(8,128)(2,1)} %bitcast.55, bf16[4,1152,128]{2,1,0:T(8,128)(2,1)} %copy-done.1, bf16[4,1152,128]{2,1,0:T(8,128)(2,1)} %collective-permute-done.3.theirs), custom_call_target="tpu_custom_call" | custom-call | tf_op jit(solution)/shard_map/reduce_conv/pallas_call | solution.py:105
  84.6 5.7 %all-to-all-start.3 = ((bf16[32,112,128]{2,1,0:T(8,128)(2,1)}), bf16[32,112,128]{2,1,0:T(8,128)(2,1)S(1)}, u32[]{:S(2)}, u32[]{:S(2)}) async-start(bf16[32,112,128]{2,1,0:T(8,128)(2,1)} %reduce_conv.1), calls=%async_computation.3 | async-start | bytes 1835008 | tf_op jit(solution)/shard_map/all_to_all | solution.py:17
  90.4 0.0 collective-permute-done.4
  90.4 25.5 %all-to-all-done.3 = bf16[32,112,128]{2,1,0:T(8,128)(2,1)S(1)} async-done(((bf16[32,112,128]{2,1,0:T(8,128)(2,1)}), bf16[32,112,128]{2,1,0:T(8,128)(2,1)S(1)}, u32[]{:S(2)}, u32[]{:S(2)}) %all-to-all-start.3) | async-done | bytes 917536 | tf_op jit(solution)/shard_map/all_to_all | solution.py:17
  115.9 0.0 copy-start.3
  115.9 0.9 copy-done.3
  116.8 7.9 %wide_conv.1 = bf16[2,8,56,128]{3,2,1,0:T(8,128)(2,1)} custom-call(s32[2]{0:T(128)} %pad_add_fusion.place, bf16[4,8,112,128]{3,2,1,0:T(8,128)(2,1)} %bitcast.56, bf16[9,1024,128]{2,1,0:T(8,128)(2,1)} %bitcast.57, bf16[9,1024,128]{2,1,0:T(8,128)(2,1)} %bitcast.25.other), custom_call_target="tpu_custom_call" | custom-call | tf_op jit(solution)/shard_map/wide_conv/pallas_call | solution.py:151
  124.7 17.9 %all_to_all.26 = bf16[16,56,128]{2,1,0:T(8,128)(2,1)S(1)} all-to-all(bf16[16,56,128]{2,1,0:T(8,128)(2,1)} %bitcast.60), channel_id=1, replica_groups=mesh['yl'=4,'core'=2,'x'=4,'yh'=2,'z'=8] {'core','x','yh'}, dimensions={0} | all-to-all | bytes 458752 | tf_op jit(solution)/shard_map/all_to_all | solution.py:17
  142.6 0.6 copy.24
  (40 shorter events, 0.7 us)
Async XLA Ops:
  0.0 13.8 %copy-start = (bf16[3,3,128,128]{3,2,1,0:T(8,128)(2,1)S(1)}, bf16[3,3,128,128]{3,2,1,0:T(8,128)(2,1)}, u32[]{:S(2)}) copy-start(bf16[3,3,128,128]{3,2,1,0:T(8,128)(2,1)} %param.5) | copy-start | bytes 884740
  0.0 27.2 %collective-permute-start.2 = (bf16[1152,128]{1,0:T(8,128)(2,1)}, bf16[1152,128]{1,0:T(8,128)(2,1)S(1)}, u32[]{:S(2)}, u32[]{:S(2)}) collective-permute-start(bf16[1152,128]{1,0:T(8,128)(2,1)} %bitcast.63), channel_id=1, source_target_pairs={{0,384},{128,0},{256,128},{384,256},{1,385},{129,1},{257,129},{385... | collective-permute-start | bytes 884744 | tf_op jit(solution)/shard_map/ppermute | solution.py:174
  2.5 24.8 %collective-permute-start.1 = (bf16[1152,128]{1,0:T(8,128)(2,1)}, bf16[1152,128]{1,0:T(8,128)(2,1)S(1)}, u32[]{:S(2)}, u32[]{:S(2)}) collective-permute-start(bf16[1152,128]{1,0:T(8,128)(2,1)} %bitcast.64), channel_id=1, source_target_pairs={{0,256},{128,384},{256,0},{384,128},{1,257},{129,385},{257,1},{385... | collective-permute-start | bytes 884744 | tf_op jit(solution)/shard_map/ppermute | solution.py:174
  7.0 29.0 %collective-permute-start = (bf16[1152,128]{1,0:T(8,128)(2,1)}, bf16[1152,128]{1,0:T(8,128)(2,1)S(1)}, u32[]{:S(2)}, u32[]{:S(2)}) collective-permute-start(bf16[1152,128]{1,0:T(8,128)(2,1)} %bitcast.65), channel_id=1, source_target_pairs={{0,128},{128,256},{256,384},{384,0},{1,129},{129,257},{257,385},{3... | collective-permute-start | bytes 884744 | tf_op jit(solution)/shard_map/ppermute | solution.py:174
  13.8 22.2 %copy-start.4 = (bf16[3,3,128,128]{3,2,1,0:T(8,128)(2,1)S(1)}, bf16[3,3,128,128]{3,2,1,0:T(8,128)(2,1)}, u32[]{:S(2)}) copy-start(bf16[3,3,128,128]{3,2,1,0:T(8,128)(2,1)} %param.6) | copy-start | bytes 884740
  15.0 25.9 %all-to-all-start = ((bf16[8,112,128]{2,1,0:T(8,128)(2,1)}), bf16[8,112,128]{2,1,0:T(8,128)(2,1)S(1)}, u32[]{:S(2)}, u32[]{:S(2)}) async-start(bf16[8,112,128]{2,1,0:T(8,128)(2,1)} %bitcast.12), calls=%async_computation | async-start | bytes 458752 | tf_op jit(solution)/shard_map/all_to_all | solution.py:17
  36.2 26.1 %copy-start.1 = (bf16[4,1152,128]{2,1,0:T(8,128)(2,1)}, bf16[4,1152,128]{2,1,0:T(8,128)(2,1)S(1)}, u32[]{:S(2)}) copy-start(bf16[4,1152,128]{2,1,0:T(8,128)(2,1)S(1)} %pad_maximum_fusion.mine) | copy-start | bytes 3538948
  36.2 32.1 %collective-permute-start.3 = (bf16[4,1152,128]{2,1,0:T(8,128)(2,1)S(1)}, bf16[4,1152,128]{2,1,0:T(8,128)(2,1)}, u32[]{:S(2)}, u32[]{:S(2)}) collective-permute-start(bf16[4,1152,128]{2,1,0:T(8,128)(2,1)S(1)} %pad_maximum_fusion.mine), channel_id=1, source_target_pairs={{0,64},{64,0},{1,65},{65,1},{2,66},{66,2},{3,67},{67,3},{4,68},{68... | collective-permute-start | bytes 3538952 | tf_op jit(solution)/shard_map/ppermute | solution.py:21
  62.2 16.5 %all-to-all-start.2 = ((bf16[4,896,128]{2,1,0:T(8,128)(2,1)}), bf16[4,896,128]{2,1,0:T(8,128)(2,1)S(1)}, u32[]{:S(2)}, u32[]{:S(2)}) async-start(bf16[4,896,128]{2,1,0:T(8,128)(2,1)} %broadcast_in_dim.24), calls=%async_computation.2 | async-start | bytes 1835008 | tf_op jit(solution)/shard_map/all_to_all | solution.py:17
  65.8 24.6 %collective-permute-start.4 = (bf16[3,3,1024,128]{3,2,1,0:T(8,128)(2,1)}, bf16[3,3,1024,128]{3,2,1,0:T(8,128)(2,1)}, u32[]{:S(2)}, u32[]{:S(2)}) collective-permute-start(bf16[3,3,1024,128]{3,2,1,0:T(8,128)(2,1)} %param.7), channel_id=1, source_target_pairs={{0,64},{64,0},{1,65},{65,1},{2,66},{66,2},{3,67},{67,3},{4,68},{68... | collective-permute-start | bytes 7077896 | tf_op jit(solution)/shard_map/ppermute | solution.py:21
  78.8 1.0 copy-start.2
  84.6 31.2 %all-to-all-start.3 = ((bf16[32,112,128]{2,1,0:T(8,128)(2,1)}), bf16[32,112,128]{2,1,0:T(8,128)(2,1)S(1)}, u32[]{:S(2)}, u32[]{:S(2)}) async-start(bf16[32,112,128]{2,1,0:T(8,128)(2,1)} %reduce_conv.1), calls=%async_computation.3 | async-start | bytes 1835008 | tf_op jit(solution)/shard_map/all_to_all | solution.py:17
  115.9 0.9 copy-start.3

commit v4 on v3

--- a/solution.py
+++ b/solution.py
@@ -43,20 +43,6 @@
             planes.append(jnp.concatenate(taps, axis=3).reshape(n * 56, 9 * c))
     table = jnp.concatenate(planes, axis=0)
     return jnp.dot(table, weight.reshape(9 * c, -1), preferred_element_type=F32)
-
-
-def nine_taps(value, rows, inner_top, inner_bottom):
-    count = value.shape[0]
-    taps = []
-    for a in range(3):
-        for b in range(3):
-            moved = value if b == 1 else rows[b]
-            if a == 0:
-                moved = jnp.where(inner_top, pltpu.roll(moved, 8, 0), 0.0)
-            elif a == 2:
-                moved = jnp.where(inner_bottom, pltpu.roll(moved, count - 8, 0), 0.0)
-            taps.append(moved.astype(BF))
-    return jnp.concatenate(taps, axis=1)
 
 
 def reduce_kernel(place, planes, mine, theirs, out, planes_v, mine_v, theirs_v, narrow, sems, out_sems):
@@ -119,48 +105,11 @@
     )(place, planes, mine, theirs)
 
 
-def wide_kernel(place, maps, own, other, out, maps_v, own_v, other_v, sems):
-    core = place[1]
-    copies = []
-    for z in range(8):
-        channels = pl.ds(128 * z, 128)
-        trio = (
-            pltpu.make_async_copy(maps.at[:, z], maps_v.at[z], sems.at[0, z]),
-            pltpu.make_async_copy(own.at[:, channels], own_v.at[z], sems.at[1, z]),
-            pltpu.make_async_copy(other.at[:, channels], other_v.at[z], sems.at[2, z]),
-        )
-        for copy in trio:
-            copy.start()
-        copies.append(trio)
-    line = lax.rem(lax.broadcasted_iota(jnp.int32, (448, 128), 0) // 8, 7)
-    total = jnp.zeros((448, 256), F32)
-    for z in range(8):
-        for copy in copies[z]:
-            copy.wait()
-        value = maps_v[z].reshape(448, 128).astype(F32)
-        rows = {0: pltpu.roll(value, 1, 0), 2: pltpu.roll(value, 447, 0)}
-        table = nine_taps(value, rows, line > 0, line < 6)
-        weight = jnp.concatenate([own_v[z].reshape(1152, 128), other_v[z].reshape(1152, 128)], axis=1)
-        total = total + jnp.dot(table, weight, preferred_element_type=F32)
-    out[core] = total[:, :128].astype(BF).reshape(8, 56, 128)
-    out[1 - core] = total[:, 128:].astype(BF).reshape(8, 56, 128)
-
-
-def wide_conv(place, maps, own, other):
-    hbm = pl.BlockSpec(memory_space=pl.ANY)
-    return pl.pallas_call(
-        wide_kernel,
-        out_shape=jax.ShapeDtypeStruct((2, 8, 56, 128), BF),
-        in_specs=[pl.BlockSpec(memory_space=pltpu.SMEM), hbm, hbm, hbm],
-        out_specs=pl.BlockSpec(memory_space=pltpu.VMEM),
-        scratch_shapes=[
-            pltpu.VMEM((8, 4, 112, 128), BF),
-            pltpu.VMEM((8, 9, 128, 128), BF),
-            pltpu.VMEM((8, 9, 128, 128), BF),
-            pltpu.SemaphoreType.DMA((3, 8)),
-        ],
-        name="wide_conv",
-    )(place, maps, own, other)
+def wide_conv(maps, weight):
+    n, _, _, c = maps.shape
+    padded = jnp.pad(maps, ((0, 0), (1, 1), (1, 1), (0, 0)))
+    table = jnp.concatenate([padded[:, a : a + 7, b : b + 8] for a in range(3) for b in range(3)], axis=3)
+    return jnp.dot(table.reshape(n * 56, 9 * c), weight, preferred_element_type=F32)
 
 
 def real_columns(values):
@@ -191,6 +140,9 @@
 
     mine, theirs = all_inputs(w_reduce)
     other = swap_cores(w_wide)
+    weight_wide = jnp.concatenate(
+        [jnp.where(core == 0, w_wide, other), jnp.where(core == 0, other, w_wide)], axis=3
+    ).reshape(9216, 256)
 
     own = lax.dynamic_slice_in_dim(images, out_block * 128, 128, 3)
     own = lax.dynamic_index_in_dim(parity_planes(own), plane, 0, keepdims=False)
@@ -205,10 +157,11 @@
     place = jnp.stack([lax.axis_index(YL), core]).astype(jnp.int32)
     narrow = reduce_conv(place, planes, mine, theirs)
 
-    gathered = exchange(narrow, (YL, Z)).reshape(4, 8, 112, 128)
-    wide = wide_conv(place, gathered, w_wide.reshape(9, 1024, 128), other.reshape(9, 1024, 128))
+    gathered = exchange(narrow, (YL, Z)).reshape(4, 8, 2, 7, 8, 128)
+    maps = jnp.concatenate([gathered[:, z] for z in range(8)], axis=4).reshape(8, 7, 8, 1024)
+    wide = wide_conv(maps, weight_wide).astype(BF).reshape(8, 56, 256)
 
-    wide = wide.reshape(16, 56, 128)
+    wide = jnp.concatenate([wide[..., :128], wide[..., 128:]], axis=0)
     wide = exchange(wide, (CORE, X, YH)).reshape(2, 8, 7, 8, 128)
     total = wide.astype(F32).sum(1).astype(BF)
     return total[:, None, :, 1:, :]

time: 144 us -> 142 us (0.986)
  waiting for transfers between devices: 52.8 us -> 44.1 us
  Pallas kernels: 12.8 us -> 4.89 us
  other arithmetic: 0.94 us -> 6.37 us
  starting transfers between devices: 31.3 us -> 35 us
  local copies, waits for them, and re-layouts: 6.65 us -> 9.69 us
  matrix products: 0.44 us -> 2.73 us
    pallas_call x1 -> x0, Pallas kernels: 7.91 us -> none  [wide_conv(): pl.pallas_call(wide_kernel, out_shape=jax.ShapeDtypeStruct((2, 8, 56, 128...]
    all_to_all x3, waiting for transfers between devices: 38.8 us -> 32.2 us  [exchange(): return lax.all_to_all(values, axes, 0, 0, tiled=True)]
    all_to_all x3, starting transfers between devices: 16.1 us -> 20.7 us  [exchange(): return lax.all_to_all(values, axes, 0, 0, tiled=True)]
    concatenate x0 -> x2, other arithmetic: none -> 2.73 us  [the longest x1 2.71 us: body(): jnp.concatenate([jnp.where(core == 0, w_wide, other), jnp.where(core == 0...]
    select_n x0 -> x1, other arithmetic: none -> 2.69 us  [body(): jnp.where(core == 0, w_wide, other)]
    dot_general x0 -> x1, matrix products: none -> 2.29 us  [wide_conv(): jnp.dot(table.reshape(n * 56, 9 * c), weight, preferred_element_type=F32)]
    ppermute x3, waiting for transfers between devices: 14 us -> 11.8 us  [all_inputs(): lax.ppermute(blocks[0], YL, [(j, (j + shift) % 4) for j in range(4)])]
    unnamed x37 -> x61, local copies, waits for them, and re-layouts: 2.27 us -> 3.73 us
  transfers between devices with their start and end apart: 8 -> 8, of which waited for: 5 -> 5; matrix products, arithmetic and copies ran while one was open for 4% -> 8% of each run, Pallas kernels for 3% -> 3%
where the time goes in v4:
time: 142 us; the launch traced here: 141 us
  waiting for transfers between devices  44.1 us (31%)
  blocking collectives  37.9 us (27%)
  starting transfers between devices  35 us (25%)
  local copies, waits for them, and re-layouts  9.69 us (7%)
  other arithmetic  6.37 us (4%)
  Pallas kernels  4.89 us (3%)
  matrix products  2.73 us (2%)
    all_to_all x2, blocking collectives, exchange(): return lax.all_to_all(values, axes, 0, 0, tiled=True)  37.9 us
    all_to_all x3, waiting for transfers between devices, exchange(): return lax.all_to_all(values, axes, 0, 0, tiled=True)  32.2 us
    all_to_all x3, starting transfers between devices, exchange(): return lax.all_to_all(values, axes, 0, 0, tiled=True)  20.7 us
    ppermute x3, waiting for transfers between devices, all_inputs(): lax.ppermute(blocks[0], YL, [(j, (j + shift) % 4) for j in range(4)])  11.8 us
    ppermute x3, starting transfers between devices, all_inputs(): lax.ppermute(blocks[0], YL, [(j, (j + shift) % 4) for j in range(4)])  10.5 us
    pallas_call x1, Pallas kernels, reduce_conv(): pl.pallas_call(reduce_kernel, out_shape=jax.ShapeDtypeStruct((32, 112, 12...  4.89 us
    ppermute x2, starting transfers between devices, swap_cores(): return lax.ppermute(values, CORE, SWAP)  3.84 us
    unnamed x61, local copies, waits for them, and re-layouts  3.73 us
  transfers between devices with their start and end apart: 8, of which 5 were waited for; matrix products, arithmetic and copies ran while one was open for 8% of the time, Pallas kernels for 3%

profile of v4, /device:TPU:72, one launch (start us, length us, event | category | flops | bytes accessed | tf_op | source)
XLA Modules:
  0.0 141.3 jit_solution(13624335202583350047)
XLA Ops:
  0.0 3.6 %collective-permute-start = (bf16[1152,128]{1,0:T(8,128)(2,1)}, bf16[1152,128]{1,0:T(8,128)(2,1)S(1)}, u32[]{:S(2)}, u32[]{:S(2)}) collective-permute-start(bf16[1152,128]{1,0:T(8,128)(2,1)} %bitcast.113), channel_id=1, source_target_pairs={{0,128},{128,256},{256,384},{384,0},{1,129},{129,257},{257,385},{3... | collective-permute-start | bytes 884744 | tf_op jit(solution)/shard_map/ppermute | solution.py:123
  3.6 3.1 %collective-permute-start.1 = (bf16[1152,128]{1,0:T(8,128)(2,1)}, bf16[1152,128]{1,0:T(8,128)(2,1)S(1)}, u32[]{:S(2)}, u32[]{:S(2)}) collective-permute-start(bf16[1152,128]{1,0:T(8,128)(2,1)} %bitcast.114), channel_id=1, source_target_pairs={{0,256},{128,384},{256,0},{384,128},{1,257},{129,385},{257,1},{385... | collective-permute-start | bytes 884744 | tf_op jit(solution)/shard_map/ppermute | solution.py:123
  6.8 3.7 %collective-permute-start.2 = (bf16[1152,128]{1,0:T(8,128)(2,1)}, bf16[1152,128]{1,0:T(8,128)(2,1)S(1)}, u32[]{:S(2)}, u32[]{:S(2)}) collective-permute-start(bf16[1152,128]{1,0:T(8,128)(2,1)} %bitcast.115), channel_id=1, source_target_pairs={{0,384},{128,0},{256,128},{384,256},{1,385},{129,1},{257,129},{385... | collective-permute-start | bytes 884744 | tf_op jit(solution)/shard_map/ppermute | solution.py:123
  10.5 1.1 constant_dynamic-slice_fusion.1
  11.7 0.4 pad_slice_fusion.15
  12.1 0.2 fusion.13
  12.9 0.4 convolution_convert_fusion.1
  13.4 0.7 broadcast_in_dim.21
  14.1 7.8 %all-to-all-start = ((bf16[8,112,128]{2,1,0:T(8,128)(2,1)}), bf16[8,112,128]{2,1,0:T(8,128)(2,1)S(1)}, u32[]{:S(2)}, u32[]{:S(2)}) async-start(bf16[8,112,128]{2,1,0:T(8,128)(2,1)} %bitcast.12), calls=%async_computation | async-start | bytes 458752 | tf_op jit(solution)/shard_map/all_to_all | solution.py:17
  21.9 1.9 %collective-permute-start.4 = (bf16[3,3,1024,128]{3,2,1,0:T(8,128)(2,1)}, bf16[3,3,1024,128]{3,2,1,0:T(8,128)(2,1)}, u32[]{:S(2)}, u32[]{:S(2)}) collective-permute-start(bf16[3,3,1024,128]{3,2,1,0:T(8,128)(2,1)} %param.7), channel_id=1, source_target_pairs={{0,64},{64,0},{1,65},{65,1},{2,66},{66,2},{3,67},{67,3},{4,68},{68... | collective-permute-start | bytes 7077896 | tf_op jit(solution)/shard_map/ppermute | solution.py:21
  23.8 0.1 copy.20
  23.9 2.5 %collective-permute-done = bf16[1152,128]{1,0:T(8,128)(2,1)S(1)} collective-permute-done((bf16[1152,128]{1,0:T(8,128)(2,1)}, bf16[1152,128]{1,0:T(8,128)(2,1)S(1)}, u32[]{:S(2)}, u32[]{:S(2)}) %collective-permute-start) | collective-permute-done | bytes 294944 | tf_op jit(solution)/shard_map/ppermute | solution.py:123
  26.4 6.1 %collective-permute-done.1 = bf16[1152,128]{1,0:T(8,128)(2,1)S(1)} collective-permute-done((bf16[1152,128]{1,0:T(8,128)(2,1)}, bf16[1152,128]{1,0:T(8,128)(2,1)S(1)}, u32[]{:S(2)}, u32[]{:S(2)}) %collective-permute-start.1) | collective-permute-done | bytes 294944 | tf_op jit(solution)/shard_map/ppermute | solution.py:123
  32.6 3.2 %collective-permute-done.2 = bf16[1152,128]{1,0:T(8,128)(2,1)S(1)} collective-permute-done((bf16[1152,128]{1,0:T(8,128)(2,1)}, bf16[1152,128]{1,0:T(8,128)(2,1)S(1)}, u32[]{:S(2)}, u32[]{:S(2)}) %collective-permute-start.2) | collective-permute-done | bytes 294944 | tf_op jit(solution)/shard_map/ppermute | solution.py:123
  35.8 0.1 pad_maximum_fusion.1.mine
  35.9 1.9 %collective-permute-start.3 = (bf16[4,1152,128]{2,1,0:T(8,128)(2,1)S(1)}, bf16[4,1152,128]{2,1,0:T(8,128)(2,1)}, u32[]{:S(2)}, u32[]{:S(2)}) collective-permute-start(bf16[4,1152,128]{2,1,0:T(8,128)(2,1)S(1)} %pad_maximum_fusion.1.mine), channel_id=1, source_target_pairs={{0,64},{64,0},{1,65},{65,1},{2,66},{66,2},{3,67},{67,3},{4,68},{68... | collective-permute-start | bytes 3538952 | tf_op jit(solution)/shard_map/ppermute | solution.py:21
  37.9 0.0 all-to-all-done
  37.9 0.1 broadcast_select_fusion.2
  38.0 20.1 %all_to_all.25 = bf16[16,56,128]{2,1,0:T(8,128)(2,1)S(1)} all-to-all(bf16[16,56,128]{2,1,0:T(8,128)(2,1)S(1)} %bitcast.110), channel_id=1, replica_groups=mesh['yl'=4,'core'=2,'x'=4,'yh'=2,'z'=8] {'core','z'}, dimensions={0} | all-to-all | bytes 458752 | tf_op jit(solution)/shard_map/all_to_all | solution.py:17
  58.2 1.1 broadcast_in_dim.24
  59.3 4.3 %all-to-all-start.2 = ((bf16[4,896,128]{2,1,0:T(8,128)(2,1)}), bf16[4,896,128]{2,1,0:T(8,128)(2,1)S(1)}, u32[]{:S(2)}, u32[]{:S(2)}) async-start(bf16[4,896,128]{2,1,0:T(8,128)(2,1)} %broadcast_in_dim.24), calls=%async_computation.2 | async-start | bytes 1835008 | tf_op jit(solution)/shard_map/all_to_all | solution.py:17
  63.6 0.6 pad_add_fusion.place
  64.2 0.0 collective-permute-done.3.theirs
  64.2 12.2 %all-to-all-done.2 = bf16[4,896,128]{2,1,0:T(8,128)(2,1)S(1)} async-done(((bf16[4,896,128]{2,1,0:T(8,128)(2,1)}), bf16[4,896,128]{2,1,0:T(8,128)(2,1)S(1)}, u32[]{:S(2)}, u32[]{:S(2)}) %all-to-all-start.2) | async-done | bytes 917536 | tf_op jit(solution)/shard_map/all_to_all | solution.py:17
  76.3 0.9 copy-done.2
  77.3 4.9 %reduce_conv.1 = bf16[32,112,128]{2,1,0:T(8,128)(2,1)} custom-call(s32[2]{0:T(128)} %pad_add_fusion.place, bf16[4,2,8,56,128]{4,3,2,1,0:T(8,128)(2,1)} %bitcast.83, bf16[4,1152,128]{2,1,0:T(8,128)(2,1)} %copy-done.1, bf16[4,1152,128]{2,1,0:T(8,128)(2,1)} %collective-permute-done.3.theirs), custom_call_target="tpu_custom_call" | custom-call | tf_op jit(solution)/shard_map/reduce_conv/pallas_call | solution.py:91
  82.2 8.6 %all-to-all-start.3 = ((bf16[32,112,128]{2,1,0:T(8,128)(2,1)}), bf16[32,112,128]{2,1,0:T(8,128)(2,1)S(1)}, u32[]{:S(2)}, u32[]{:S(2)}) async-start(bf16[32,112,128]{2,1,0:T(8,128)(2,1)} %reduce_conv.1), calls=%async_computation.3 | async-start | bytes 1835008 | tf_op jit(solution)/shard_map/all_to_all | solution.py:17
  90.8 0.0 collective-permute-done.4
  90.8 2.7 %broadcast_select_fusion.1 = (bf16[3,3,1024,128]{3,2,1,0:T(8,128)(2,1)S(1)}, bf16[3,3,1024,128]{3,2,1,0:T(8,128)(2,1)S(1)}) fusion(bf16[3,3,1024,128]{3,2,1,0:T(8,128)(2,1)} %param.7, bf16[3,3,1024,128]{3,2,1,0:T(8,128)(2,1)} %collective-permute-done.4, pred[]{:T(512)S(6)} %eq.4), kind=kLoop, calls=%fused_computation.10 | loop fusion | flops 2359296 | bytes 9437185 | tf_op jit(solution)/shard_map/jit(_where)/select_n | solution.py:144
  93.5 2.7 %pad_maximum_fusion = bf16[3,3,1024,256]{3,2,1,0:T(8,128)(2,1)} fusion(bf16[3,3,1024,128]{3,2,1,0:T(8,128)(2,1)S(1)} %get-tuple-element.6, bf16[3,3,1024,128]{3,2,1,0:T(8,128)(2,1)S(1)} %get-tuple-element.5), kind=kLoop, calls=%fused_computation.8 | loop fusion | flops 9437184 | bytes 9437184 | tf_op jit(solution)/shard_map/concatenate | solution.py:143
  96.2 20.1 %all-to-all-done.3 = bf16[32,112,128]{2,1,0:T(8,128)(2,1)S(1)} async-done(((bf16[32,112,128]{2,1,0:T(8,128)(2,1)}), bf16[32,112,128]{2,1,0:T(8,128)(2,1)S(1)}, u32[]{:S(2)}, u32[]{:S(2)}) %all-to-all-start.3) | async-done | bytes 917536 | tf_op jit(solution)/shard_map/all_to_all | solution.py:17
  116.3 0.1 fusion.11
  116.7 1.3 pad_slice_fusion
  118.1 0.0 slice-start
  118.1 0.1 constant_dynamic-update-slice_fusion.59
  118.1 0.1 constant_dynamic-update-slice_fusion.58
  118.2 0.1 constant_dynamic-update-slice_fusion.57
  118.3 0.1 constant_dynamic-update-slice_fusion.56
  118.5 0.0 slice-start.1
  118.7 0.1 constant_dynamic-update-slice_fusion.47
  118.8 0.1 constant_dynamic-update-slice_fusion.46
  118.8 0.1 constant_dynamic-update-slice_fusion.45
  118.9 0.1 constant_dynamic-update-slice_fusion.44
  119.0 1.3 slice-done
  120.2 0.2 slice-done.1
  120.5 2.3 %convolution_convert_fusion = bf16[448,256]{1,0:T(8,128)(2,1)S(1)} fusion(bf16[448,9216]{1,0:T(8,128)(2,1)S(1)} %constant_dynamic-update-slice_fusion.44, bf16[9216,256]{1,0:T(8,128)(2,1)S(1)} %bitcast.80), kind=kOutput, calls=%fused_computation.11 | convolution fusion | flops 2114043904 | bytes 13205504 | tf_op jit(solution)/shard_map/dot_general | solution.py:112
  122.8 17.8 %all_to_all.26 = bf16[16,56,128]{2,1,0:T(8,128)(2,1)S(1)} all-to-all(bf16[16,56,128]{2,1,0:T(8,128)(2,1)S(1)} %pad_maximum_fusion.2), channel_id=1, replica_groups=mesh['yl'=4,'core'=2,'x'=4,'yh'=2,'z'=8] {'core','x','yh'}, dimensions={0} | all-to-all | bytes 458752 | tf_op jit(solution)/shard_map/all_to_all | solution.py:17
  140.7 0.6 copy.24
  (66 shorter events, 1.3 us)
Async XLA Ops:
  0.0 12.9 %copy-start = (bf16[3,3,128,128]{3,2,1,0:T(8,128)(2,1)S(1)}, bf16[3,3,128,128]{3,2,1,0:T(8,128)(2,1)}, u32[]{:S(2)}) copy-start(bf16[3,3,128,128]{3,2,1,0:T(8,128)(2,1)} %param.5) | copy-start | bytes 884740
  0.0 35.7 %copy-start.3 = (bf16[3,3,128,128]{3,2,1,0:T(8,128)(2,1)S(1)}, bf16[3,3,128,128]{3,2,1,0:T(8,128)(2,1)}, u32[]{:S(2)}) copy-start(bf16[3,3,128,128]{3,2,1,0:T(8,128)(2,1)} %param.6) | copy-start | bytes 884740
  0.0 26.4 %collective-permute-start = (bf16[1152,128]{1,0:T(8,128)(2,1)}, bf16[1152,128]{1,0:T(8,128)(2,1)S(1)}, u32[]{:S(2)}, u32[]{:S(2)}) collective-permute-start(bf16[1152,128]{1,0:T(8,128)(2,1)} %bitcast.113), channel_id=1, source_target_pairs={{0,128},{128,256},{256,384},{384,0},{1,129},{129,257},{257,385},{3... | collective-permute-start | bytes 884744 | tf_op jit(solution)/shard_map/ppermute | solution.py:123
  3.6 29.0 %collective-permute-start.1 = (bf16[1152,128]{1,0:T(8,128)(2,1)}, bf16[1152,128]{1,0:T(8,128)(2,1)S(1)}, u32[]{:S(2)}, u32[]{:S(2)}) collective-permute-start(bf16[1152,128]{1,0:T(8,128)(2,1)} %bitcast.114), channel_id=1, source_target_pairs={{0,256},{128,384},{256,0},{384,128},{1,257},{129,385},{257,1},{385... | collective-permute-start | bytes 884744 | tf_op jit(solution)/shard_map/ppermute | solution.py:123
  6.8 29.0 %collective-permute-start.2 = (bf16[1152,128]{1,0:T(8,128)(2,1)}, bf16[1152,128]{1,0:T(8,128)(2,1)S(1)}, u32[]{:S(2)}, u32[]{:S(2)}) collective-permute-start(bf16[1152,128]{1,0:T(8,128)(2,1)} %bitcast.115), channel_id=1, source_target_pairs={{0,384},{128,0},{256,128},{384,256},{1,385},{129,1},{257,129},{385... | collective-permute-start | bytes 884744 | tf_op jit(solution)/shard_map/ppermute | solution.py:123
  14.1 23.7 %all-to-all-start = ((bf16[8,112,128]{2,1,0:T(8,128)(2,1)}), bf16[8,112,128]{2,1,0:T(8,128)(2,1)S(1)}, u32[]{:S(2)}, u32[]{:S(2)}) async-start(bf16[8,112,128]{2,1,0:T(8,128)(2,1)} %bitcast.12), calls=%async_computation | async-start | bytes 458752 | tf_op jit(solution)/shard_map/all_to_all | solution.py:17
  21.9 68.9 %collective-permute-start.4 = (bf16[3,3,1024,128]{3,2,1,0:T(8,128)(2,1)}, bf16[3,3,1024,128]{3,2,1,0:T(8,128)(2,1)}, u32[]{:S(2)}, u32[]{:S(2)}) collective-permute-start(bf16[3,3,1024,128]{3,2,1,0:T(8,128)(2,1)} %param.7), channel_id=1, source_target_pairs={{0,64},{64,0},{1,65},{65,1},{2,66},{66,2},{3,67},{67,3},{4,68},{68... | collective-permute-start | bytes 7077896 | tf_op jit(solution)/shard_map/ppermute | solution.py:21
  35.9 40.4 %copy-start.1 = (bf16[4,1152,128]{2,1,0:T(8,128)(2,1)}, bf16[4,1152,128]{2,1,0:T(8,128)(2,1)S(1)}, u32[]{:S(2)}) copy-start(bf16[4,1152,128]{2,1,0:T(8,128)(2,1)S(1)} %pad_maximum_fusion.1.mine) | copy-start | bytes 3538948
  35.9 28.3 %collective-permute-start.3 = (bf16[4,1152,128]{2,1,0:T(8,128)(2,1)S(1)}, bf16[4,1152,128]{2,1,0:T(8,128)(2,1)}, u32[]{:S(2)}, u32[]{:S(2)}) collective-permute-start(bf16[4,1152,128]{2,1,0:T(8,128)(2,1)S(1)} %pad_maximum_fusion.1.mine), channel_id=1, source_target_pairs={{0,64},{64,0},{1,65},{65,1},{2,66},{66,2},{3,67},{67,3},{4,68},{68... | collective-permute-start | bytes 3538952 | tf_op jit(solution)/shard_map/ppermute | solution.py:21
  59.3 17.1 %all-to-all-start.2 = ((bf16[4,896,128]{2,1,0:T(8,128)(2,1)}), bf16[4,896,128]{2,1,0:T(8,128)(2,1)S(1)}, u32[]{:S(2)}, u32[]{:S(2)}) async-start(bf16[4,896,128]{2,1,0:T(8,128)(2,1)} %broadcast_in_dim.24), calls=%async_computation.2 | async-start | bytes 1835008 | tf_op jit(solution)/shard_map/all_to_all | solution.py:17
  76.3 0.9 copy-start.2
  82.2 34.1 %all-to-all-start.3 = ((bf16[32,112,128]{2,1,0:T(8,128)(2,1)}), bf16[32,112,128]{2,1,0:T(8,128)(2,1)S(1)}, u32[]{:S(2)}, u32[]{:S(2)}) async-start(bf16[32,112,128]{2,1,0:T(8,128)(2,1)} %reduce_conv.1), calls=%async_computation.3 | async-start | bytes 1835008 | tf_op jit(solution)/shard_map/all_to_all | solution.py:17
  118.1 2.2 %slice-start = ((s8[4718592]{0:T(1024)(128)(4,1)}), s8[4194304]{0:T(1024)(128)(4,1)S(1)}, s32[]{:S(2)}) async-start(s8[4718592]{0:T(1024)(128)(4,1)} %bitcast.78), calls=%async_computation.5 | async-start | bytes 8388608
  118.5 2.0 %slice-start.1 = ((s8[4718592]{0:T(1024)(128)(4,1)}), s8[524288]{0:T(1024)(128)(4,1)S(1)}, s32[]{:S(2)}) async-start(s8[4718592]{0:T(1024)(128)(4,1)} %bitcast.78), calls=%async_computation.6 | async-start | bytes 1048576

commit v5 on v4

--- a/solution.py
+++ b/solution.py
@@ -140,9 +140,7 @@
 
     mine, theirs = all_inputs(w_reduce)
     other = swap_cores(w_wide)
-    weight_wide = jnp.concatenate(
-        [jnp.where(core == 0, w_wide, other), jnp.where(core == 0, other, w_wide)], axis=3
-    ).reshape(9216, 256)
+    weight_wide = jnp.concatenate([w_wide, other], axis=3).reshape(9216, 256)
 
     own = lax.dynamic_slice_in_dim(images, out_block * 128, 128, 3)
     own = lax.dynamic_index_in_dim(parity_planes(own), plane, 0, keepdims=False)
@@ -161,7 +159,8 @@
     maps = jnp.concatenate([gathered[:, z] for z in range(8)], axis=4).reshape(8, 7, 8, 1024)
     wide = wide_conv(maps, weight_wide).astype(BF).reshape(8, 56, 256)
 
-    wide = jnp.concatenate([wide[..., :128], wide[..., 128:]], axis=0)
+    mine, other = wide[..., :128], wide[..., 128:]
+    wide = jnp.concatenate([jnp.where(core == 0, mine, other), jnp.where(core == 0, other, mine)], axis=0)
     wide = exchange(wide, (CORE, X, YH)).reshape(2, 8, 7, 8, 128)
     total = wide.astype(F32).sum(1).astype(BF)
     return total[:, None, :, 1:, :]

time: 142 us -> 143 us (level)
  blocking collectives: 37.9 us -> 17.8 us
  waiting for transfers between devices: 44.1 us -> 54.5 us
  starting transfers between devices: 35 us -> 45.2 us
    all_to_all x2 -> x1, blocking collectives: 37.9 us -> 17.8 us  [exchange(): return lax.all_to_all(values, axes, 0, 0, tiled=True)]
    all_to_all x3 -> x4, starting transfers between devices: 20.7 us -> 30.8 us  [exchange(): return lax.all_to_all(values, axes, 0, 0, tiled=True)]
    all_to_all x3 -> x4, waiting for transfers between devices: 32.2 us -> 40.7 us  [exchange(): return lax.all_to_all(values, axes, 0, 0, tiled=True)]
    select_n x1, other arithmetic: 2.69 us -> 0.02 us  [body(): jnp.where(core == 0, mine, other)]
    concatenate x2, other arithmetic: 2.73 us -> 5.11 us  [the longest x1 5.08 us: body(): weight_wide = jnp.concatenate([w_wide, other], axis=3).reshape(9216, 256)]
    ppermute x3, waiting for transfers between devices: 11.8 us -> 13.7 us  [all_inputs(): lax.ppermute(blocks[0], YL, [(j, (j + shift) % 4) for j in range(4)])]
  transfers between devices with their start and end apart: 8 -> 9, of which waited for: 5 -> 6; matrix products, arithmetic and copies ran while one was open for 8% -> 8% of each run, Pallas kernels for 3% -> 3%
where the time goes in v5:
time: 143 us; the launch traced here: 142 us
  waiting for transfers between devices  54.5 us (38%)
  starting transfers between devices  45.2 us (32%)
  blocking collectives  17.8 us (12%)
  local copies, waits for them, and re-layouts  10.3 us (7%)
  other arithmetic  6.13 us (4%)
  Pallas kernels  4.9 us (3%)
  matrix products  2.73 us (2%)
    all_to_all x4, waiting for transfers between devices, exchange(): return lax.all_to_all(values, axes, 0, 0, tiled=True)  40.7 us
    all_to_all x4, starting transfers between devices, exchange(): return lax.all_to_all(values, axes, 0, 0, tiled=True)  30.8 us
    all_to_all x1, blocking collectives, exchange(): return lax.all_to_all(values, axes, 0, 0, tiled=True)  17.8 us
    ppermute x3, waiting for transfers between devices, all_inputs(): lax.ppermute(blocks[0], YL, [(j, (j + shift) % 4) for j in range(4)])  13.7 us
    ppermute x3, starting transfers between devices, all_inputs(): lax.ppermute(blocks[0], YL, [(j, (j + shift) % 4) for j in range(4)])  10.5 us
    concatenate x1, other arithmetic, body(): weight_wide = jnp.concatenate([w_wide, other], axis=3).reshape(9216, 256)  5.08 us
    pallas_call x1, Pallas kernels, reduce_conv(): pl.pallas_call(reduce_kernel, out_shape=jax.ShapeDtypeStruct((32, 112, 12...  4.9 us
    ppermute x2, starting transfers between devices, swap_cores(): return lax.ppermute(values, CORE, SWAP)  3.95 us
  transfers between devices with their start and end apart: 9, of which 6 were waited for; matrix products, arithmetic and copies ran while one was open for 8% of the time, Pallas kernels for 3%

profile of v5, /device:TPU:72, one launch (start us, length us, event | category | flops | bytes accessed | tf_op | source)
XLA Modules:
  0.0 142.2 jit_solution(5490865226747415924)
XLA Ops:
  0.0 3.6 %collective-permute-start = (bf16[1152,128]{1,0:T(8,128)(2,1)}, bf16[1152,128]{1,0:T(8,128)(2,1)S(1)}, u32[]{:S(2)}, u32[]{:S(2)}) collective-permute-start(bf16[1152,128]{1,0:T(8,128)(2,1)} %bitcast.112), channel_id=1, source_target_pairs={{0,128},{128,256},{256,384},{384,0},{1,129},{129,257},{257,385},{3... | collective-permute-start | bytes 884744 | tf_op jit(solution)/shard_map/ppermute | solution.py:123
  3.6 3.1 %collective-permute-start.1 = (bf16[1152,128]{1,0:T(8,128)(2,1)}, bf16[1152,128]{1,0:T(8,128)(2,1)S(1)}, u32[]{:S(2)}, u32[]{:S(2)}) collective-permute-start(bf16[1152,128]{1,0:T(8,128)(2,1)} %bitcast.113), channel_id=1, source_target_pairs={{0,256},{128,384},{256,0},{384,128},{1,257},{129,385},{257,1},{385... | collective-permute-start | bytes 884744 | tf_op jit(solution)/shard_map/ppermute | solution.py:123
  6.8 3.7 %collective-permute-start.2 = (bf16[1152,128]{1,0:T(8,128)(2,1)}, bf16[1152,128]{1,0:T(8,128)(2,1)S(1)}, u32[]{:S(2)}, u32[]{:S(2)}) collective-permute-start(bf16[1152,128]{1,0:T(8,128)(2,1)} %bitcast.114), channel_id=1, source_target_pairs={{0,384},{128,0},{256,128},{384,256},{1,385},{129,1},{257,129},{385... | collective-permute-start | bytes 884744 | tf_op jit(solution)/shard_map/ppermute | solution.py:123
  10.5 1.1 constant_dynamic-slice_fusion.1
  11.7 0.4 pad_slice_fusion.15
  12.1 0.2 fusion.12
  12.9 0.4 convolution_convert_fusion.1
  13.4 0.7 broadcast_in_dim.21
  14.1 7.8 %all-to-all-start = ((bf16[8,112,128]{2,1,0:T(8,128)(2,1)}), bf16[8,112,128]{2,1,0:T(8,128)(2,1)S(1)}, u32[]{:S(2)}, u32[]{:S(2)}) async-start(bf16[8,112,128]{2,1,0:T(8,128)(2,1)} %bitcast.12), calls=%async_computation | async-start | bytes 458752 | tf_op jit(solution)/shard_map/all_to_all | solution.py:17
  21.9 0.1 copy.20
  22.0 4.4 %collective-permute-done = bf16[1152,128]{1,0:T(8,128)(2,1)S(1)} collective-permute-done((bf16[1152,128]{1,0:T(8,128)(2,1)}, bf16[1152,128]{1,0:T(8,128)(2,1)S(1)}, u32[]{:S(2)}, u32[]{:S(2)}) %collective-permute-start) | collective-permute-done | bytes 294944 | tf_op jit(solution)/shard_map/ppermute | solution.py:123
  26.4 6.1 %collective-permute-done.1 = bf16[1152,128]{1,0:T(8,128)(2,1)S(1)} collective-permute-done((bf16[1152,128]{1,0:T(8,128)(2,1)}, bf16[1152,128]{1,0:T(8,128)(2,1)S(1)}, u32[]{:S(2)}, u32[]{:S(2)}) %collective-permute-start.1) | collective-permute-done | bytes 294944 | tf_op jit(solution)/shard_map/ppermute | solution.py:123
  32.6 3.2 %collective-permute-done.2 = bf16[1152,128]{1,0:T(8,128)(2,1)S(1)} collective-permute-done((bf16[1152,128]{1,0:T(8,128)(2,1)}, bf16[1152,128]{1,0:T(8,128)(2,1)S(1)}, u32[]{:S(2)}, u32[]{:S(2)}) %collective-permute-start.2) | collective-permute-done | bytes 294944 | tf_op jit(solution)/shard_map/ppermute | solution.py:123
  35.8 0.1 pad_maximum_fusion.1.mine
  35.9 1.9 %collective-permute-start.3 = (bf16[4,1152,128]{2,1,0:T(8,128)(2,1)S(1)}, bf16[4,1152,128]{2,1,0:T(8,128)(2,1)}, u32[]{:S(2)}, u32[]{:S(2)}) collective-permute-start(bf16[4,1152,128]{2,1,0:T(8,128)(2,1)S(1)} %pad_maximum_fusion.1.mine), channel_id=1, source_target_pairs={{0,64},{64,0},{1,65},{65,1},{2,66},{66,2},{3,67},{67,3},{4,68},{68... | collective-permute-start | bytes 3538952 | tf_op jit(solution)/shard_map/ppermute | solution.py:21
  37.9 0.0 all-to-all-done
  37.9 0.1 broadcast_select_fusion.2
  38.0 0.7 broadcast_in_dim.23
  38.7 10.1 %all-to-all-start.1 = ((bf16[16,56,128]{2,1,0:T(8,128)(2,1)}), bf16[16,56,128]{2,1,0:T(8,128)(2,1)S(1)}, u32[]{:S(2)}, u32[]{:S(2)}) async-start(bf16[16,56,128]{2,1,0:T(8,128)(2,1)} %bitcast.15), calls=%async_computation.1 | async-start | bytes 458752 | tf_op jit(solution)/shard_map/all_to_all | solution.py:17
  48.8 2.0 %collective-permute-start.4 = (bf16[3,3,1024,128]{3,2,1,0:T(8,128)(2,1)}, bf16[3,3,1024,128]{3,2,1,0:T(8,128)(2,1)}, u32[]{:S(2)}, u32[]{:S(2)}) collective-permute-start(bf16[3,3,1024,128]{3,2,1,0:T(8,128)(2,1)} %param.7), channel_id=1, source_target_pairs={{0,64},{64,0},{1,65},{65,1},{2,66},{66,2},{3,67},{67,3},{4,68},{68... | collective-permute-start | bytes 7077896 | tf_op jit(solution)/shard_map/ppermute | solution.py:21
  50.9 8.2 %all-to-all-done.1 = bf16[16,56,128]{2,1,0:T(8,128)(2,1)S(1)} async-done(((bf16[16,56,128]{2,1,0:T(8,128)(2,1)}), bf16[16,56,128]{2,1,0:T(8,128)(2,1)S(1)}, u32[]{:S(2)}, u32[]{:S(2)}) %all-to-all-start.1) | async-done | bytes 229408 | tf_op jit(solution)/shard_map/all_to_all | solution.py:17
  59.1 1.1 broadcast_in_dim.24
  60.1 4.3 %all-to-all-start.2 = ((bf16[4,896,128]{2,1,0:T(8,128)(2,1)}), bf16[4,896,128]{2,1,0:T(8,128)(2,1)S(1)}, u32[]{:S(2)}, u32[]{:S(2)}) async-start(bf16[4,896,128]{2,1,0:T(8,128)(2,1)} %broadcast_in_dim.24), calls=%async_computation.2 | async-start | bytes 1835008 | tf_op jit(solution)/shard_map/all_to_all | solution.py:17
  64.4 0.7 pad_add_fusion.place
  65.1 0.0 collective-permute-done.3.theirs
  65.1 12.1 %all-to-all-done.2 = bf16[4,896,128]{2,1,0:T(8,128)(2,1)S(1)} async-done(((bf16[4,896,128]{2,1,0:T(8,128)(2,1)}), bf16[4,896,128]{2,1,0:T(8,128)(2,1)S(1)}, u32[]{:S(2)}, u32[]{:S(2)}) %all-to-all-start.2) | async-done | bytes 917536 | tf_op jit(solution)/shard_map/all_to_all | solution.py:17
  77.2 0.9 copy-done.2
  78.1 4.9 %reduce_conv.1 = bf16[32,112,128]{2,1,0:T(8,128)(2,1)} custom-call(s32[2]{0:T(128)} %pad_add_fusion.place, bf16[4,2,8,56,128]{4,3,2,1,0:T(8,128)(2,1)} %bitcast.83, bf16[4,1152,128]{2,1,0:T(8,128)(2,1)} %copy-done.1, bf16[4,1152,128]{2,1,0:T(8,128)(2,1)} %collective-permute-done.3.theirs), custom_call_target="tpu_custom_call" | custom-call | tf_op jit(solution)/shard_map/reduce_conv/pallas_call | solution.py:91
  83.1 8.6 %all-to-all-start.3 = ((bf16[32,112,128]{2,1,0:T(8,128)(2,1)}), bf16[32,112,128]{2,1,0:T(8,128)(2,1)S(1)}, u32[]{:S(2)}, u32[]{:S(2)}) async-start(bf16[32,112,128]{2,1,0:T(8,128)(2,1)} %reduce_conv.1), calls=%async_computation.3 | async-start | bytes 1835008 | tf_op jit(solution)/shard_map/all_to_all | solution.py:17
  91.7 5.1 %pad_maximum_fusion = bf16[3,3,1024,256]{3,2,1,0:T(8,128)(2,1)} fusion(bf16[3,3,1024,128]{3,2,1,0:T(8,128)(2,1)} %collective-permute-done.4, bf16[3,3,1024,128]{3,2,1,0:T(8,128)(2,1)} %param.7), kind=kLoop, calls=%fused_computation.8 | loop fusion | flops 9437184 | bytes 9437184 | tf_op jit(solution)/shard_map/concatenate | solution.py:143
  96.8 20.4 %all-to-all-done.3 = bf16[32,112,128]{2,1,0:T(8,128)(2,1)S(1)} async-done(((bf16[32,112,128]{2,1,0:T(8,128)(2,1)}), bf16[32,112,128]{2,1,0:T(8,128)(2,1)S(1)}, u32[]{:S(2)}, u32[]{:S(2)}) %all-to-all-start.3) | async-done | bytes 917536 | tf_op jit(solution)/shard_map/all_to_all | solution.py:17
  117.2 0.1 fusion.11
  117.6 1.3 pad_slice_fusion
  119.0 0.0 slice-start
  119.0 0.1 constant_dynamic-update-slice_fusion.59
  119.0 0.1 constant_dynamic-update-slice_fusion.58
  119.1 0.1 constant_dynamic-update-slice_fusion.57
  119.2 0.1 constant_dynamic-update-slice_fusion.56
  119.4 0.0 slice-start.1
  119.6 0.1 constant_dynamic-update-slice_fusion.47
  119.6 0.1 constant_dynamic-update-slice_fusion.46
  119.7 0.1 constant_dynamic-update-slice_fusion.45
  119.8 0.1 constant_dynamic-update-slice_fusion.44
  119.9 1.3 slice-done
  121.1 0.2 slice-done.1
  121.4 2.3 %convolution_convert_fusion = bf16[448,256]{1,0:T(8,128)(2,1)S(1)} fusion(bf16[448,9216]{1,0:T(8,128)(2,1)S(1)} %constant_dynamic-update-slice_fusion.44, bf16[9216,256]{1,0:T(8,128)(2,1)S(1)} %bitcast.80), kind=kOutput, calls=%fused_computation.9 | convolution fusion | flops 2114043904 | bytes 13205504 | tf_op jit(solution)/shard_map/dot_general | solution.py:112
  123.7 17.8 %all_to_all.25 = bf16[16,56,128]{2,1,0:T(8,128)(2,1)S(1)} all-to-all(bf16[16,56,128]{2,1,0:T(8,128)(2,1)S(1)} %pad_maximum_fusion.2), channel_id=1, replica_groups=mesh['yl'=4,'core'=2,'x'=4,'yh'=2,'z'=8] {'core','x','yh'}, dimensions={0} | all-to-all | bytes 458752 | tf_op jit(solution)/shard_map/all_to_all | solution.py:17
  141.6 0.6 copy.24
  (66 shorter events, 1.2 us)
Async XLA Ops:
  0.0 12.9 %copy-start = (bf16[3,3,128,128]{3,2,1,0:T(8,128)(2,1)S(1)}, bf16[3,3,128,128]{3,2,1,0:T(8,128)(2,1)}, u32[]{:S(2)}) copy-start(bf16[3,3,128,128]{3,2,1,0:T(8,128)(2,1)} %param.5) | copy-start | bytes 884740
  0.0 35.7 %copy-start.3 = (bf16[3,3,128,128]{3,2,1,0:T(8,128)(2,1)S(1)}, bf16[3,3,128,128]{3,2,1,0:T(8,128)(2,1)}, u32[]{:S(2)}) copy-start(bf16[3,3,128,128]{3,2,1,0:T(8,128)(2,1)} %param.6) | copy-start | bytes 884740
  0.0 26.4 %collective-permute-start = (bf16[1152,128]{1,0:T(8,128)(2,1)}, bf16[1152,128]{1,0:T(8,128)(2,1)S(1)}, u32[]{:S(2)}, u32[]{:S(2)}) collective-permute-start(bf16[1152,128]{1,0:T(8,128)(2,1)} %bitcast.112), channel_id=1, source_target_pairs={{0,128},{128,256},{256,384},{384,0},{1,129},{129,257},{257,385},{3... | collective-permute-start | bytes 884744 | tf_op jit(solution)/shard_map/ppermute | solution.py:123
  3.6 29.0 %collective-permute-start.1 = (bf16[1152,128]{1,0:T(8,128)(2,1)}, bf16[1152,128]{1,0:T(8,128)(2,1)S(1)}, u32[]{:S(2)}, u32[]{:S(2)}) collective-permute-start(bf16[1152,128]{1,0:T(8,128)(2,1)} %bitcast.113), channel_id=1, source_target_pairs={{0,256},{128,384},{256,0},{384,128},{1,257},{129,385},{257,1},{385... | collective-permute-start | bytes 884744 | tf_op jit(solution)/shard_map/ppermute | solution.py:123
  6.8 29.0 %collective-permute-start.2 = (bf16[1152,128]{1,0:T(8,128)(2,1)}, bf16[1152,128]{1,0:T(8,128)(2,1)S(1)}, u32[]{:S(2)}, u32[]{:S(2)}) collective-permute-start(bf16[1152,128]{1,0:T(8,128)(2,1)} %bitcast.114), channel_id=1, source_target_pairs={{0,384},{128,0},{256,128},{384,256},{1,385},{129,1},{257,129},{385... | collective-permute-start | bytes 884744 | tf_op jit(solution)/shard_map/ppermute | solution.py:123
  14.1 23.7 %all-to-all-start = ((bf16[8,112,128]{2,1,0:T(8,128)(2,1)}), bf16[8,112,128]{2,1,0:T(8,128)(2,1)S(1)}, u32[]{:S(2)}, u32[]{:S(2)}) async-start(bf16[8,112,128]{2,1,0:T(8,128)(2,1)} %bitcast.12), calls=%async_computation | async-start | bytes 458752 | tf_op jit(solution)/shard_map/all_to_all | solution.py:17
  35.9 41.3 %copy-start.1 = (bf16[4,1152,128]{2,1,0:T(8,128)(2,1)}, bf16[4,1152,128]{2,1,0:T(8,128)(2,1)S(1)}, u32[]{:S(2)}) copy-start(bf16[4,1152,128]{2,1,0:T(8,128)(2,1)S(1)} %pad_maximum_fusion.1.mine) | copy-start | bytes 3538948
  35.9 29.2 %collective-permute-start.3 = (bf16[4,1152,128]{2,1,0:T(8,128)(2,1)S(1)}, bf16[4,1152,128]{2,1,0:T(8,128)(2,1)}, u32[]{:S(2)}, u32[]{:S(2)}) collective-permute-start(bf16[4,1152,128]{2,1,0:T(8,128)(2,1)S(1)} %pad_maximum_fusion.1.mine), channel_id=1, source_target_pairs={{0,64},{64,0},{1,65},{65,1},{2,66},{66,2},{3,67},{67,3},{4,68},{68... | collective-permute-start | bytes 3538952 | tf_op jit(solution)/shard_map/ppermute | solution.py:21
  38.7 20.3 %all-to-all-start.1 = ((bf16[16,56,128]{2,1,0:T(8,128)(2,1)}), bf16[16,56,128]{2,1,0:T(8,128)(2,1)S(1)}, u32[]{:S(2)}, u32[]{:S(2)}) async-start(bf16[16,56,128]{2,1,0:T(8,128)(2,1)} %bitcast.15), calls=%async_computation.1 | async-start | bytes 458752 | tf_op jit(solution)/shard_map/all_to_all | solution.py:17
  48.8 42.9 %collective-permute-start.4 = (bf16[3,3,1024,128]{3,2,1,0:T(8,128)(2,1)}, bf16[3,3,1024,128]{3,2,1,0:T(8,128)(2,1)}, u32[]{:S(2)}, u32[]{:S(2)}) collective-permute-start(bf16[3,3,1024,128]{3,2,1,0:T(8,128)(2,1)} %param.7), channel_id=1, source_target_pairs={{0,64},{64,0},{1,65},{65,1},{2,66},{66,2},{3,67},{67,3},{4,68},{68... | collective-permute-start | bytes 7077896 | tf_op jit(solution)/shard_map/ppermute | solution.py:21
  60.1 17.1 %all-to-all-start.2 = ((bf16[4,896,128]{2,1,0:T(8,128)(2,1)}), bf16[4,896,128]{2,1,0:T(8,128)(2,1)S(1)}, u32[]{:S(2)}, u32[]{:S(2)}) async-start(bf16[4,896,128]{2,1,0:T(8,128)(2,1)} %broadcast_in_dim.24), calls=%async_computation.2 | async-start | bytes 1835008 | tf_op jit(solution)/shard_map/all_to_all | solution.py:17
  77.2 0.9 copy-start.2
  83.1 34.1 %all-to-all-start.3 = ((bf16[32,112,128]{2,1,0:T(8,128)(2,1)}), bf16[32,112,128]{2,1,0:T(8,128)(2,1)S(1)}, u32[]{:S(2)}, u32[]{:S(2)}) async-start(bf16[32,112,128]{2,1,0:T(8,128)(2,1)} %reduce_conv.1), calls=%async_computation.3 | async-start | bytes 1835008 | tf_op jit(solution)/shard_map/all_to_all | solution.py:17
  119.0 2.2 %slice-start = ((s8[4718592]{0:T(1024)(128)(4,1)}), s8[4194304]{0:T(1024)(128)(4,1)S(1)}, s32[]{:S(2)}) async-start(s8[4718592]{0:T(1024)(128)(4,1)} %bitcast.78), calls=%async_computation.5 | async-start | bytes 8388608
  119.4 2.0 %slice-start.1 = ((s8[4718592]{0:T(1024)(128)(4,1)}), s8[524288]{0:T(1024)(128)(4,1)S(1)}, s32[]{:S(2)}) async-start(s8[4718592]{0:T(1024)(128)(4,1)} %bitcast.78), calls=%async_computation.6 | async-start | bytes 1048576
